TPU v7x, 128 devices: a whole 4x4x4 slice. The times are simulated.
128 devices in a mesh: row: 8 (over y_hi, z), col: 16 (over x, y_lo, core).
Axes of the slice: x: 4, y: 4 (y_hi: 2, y_lo: 2; y = y_hi * 2 + y_lo), z: 4, core: 2. Of those that a mesh axis runs over, the one named last changes fastest.
Arguments:
- images: bfloat16 [128, 3, 128, 192], P(('row', 'col')), may hold values from -1000 to 1000
- weights: bfloat16 [32, 48, 128, 1200], P('row', 'col'), may hold values from -0.1875 to 0.1875
Outputs:
- weight_grad: float32 [32, 48, 128, 1200], P('row', 'col')
All inputs are finite; a program needn't handle non-finite values.
Results may differ from a plain program's by a relative error of at most 0.006.
Values may be sent and summed in bfloat16 or wider, within the bound.
A program may use at most 128 MiB of HBM per device.

v0:
```python
import jax
import jax.numpy as jnp
from jax import lax
from jax.experimental import pallas as pl
from jax.experimental.pallas import tpu as pltpu
from jax.sharding import PartitionSpec as P

MESH = pl.DeviceIdType.MESH
F32 = jnp.float32
BF16 = jnp.bfloat16

ROWS, COLS = 8, 16
DEVS = ROWS * COLS
CH, S, FIELD, PAD = 3, 4, 20, 8
K = 1200
F = 128
B = 128
HEIGHT, WIDTH = 128, 192
PR, PC = 4, 3
SPARSITY = 0.5
EPS = 1e-05

DIRS = [(dr, dc) for dr in (-1, 0, 1) for dc in (-1, 0, 1) if (dr, dc) != (0, 0)]
OPP = [DIRS.index((-dr, -dc)) for dr, dc in DIRS]
ORDER = sorted(range(8), key=lambda k: DIRS[k][1] != 0)


def rim_rows(k):
    dr, dc = DIRS[k]
    ny = 16 if dr == 0 else 8
    nx = 16 if dc == 0 else 8
    return ny, nx


def rim(d, starts, wide):
    return (8, 16) if d == 0 else (starts[d], wide)


def outer(k):
    dr, dc = DIRS[k]
    y0 = {-1: 0, 0: 8, 1: 24}[dr]
    x0 = {-1: 0, 0: 8, 1: 20}[dc]
    ny, nx = rim_rows(k)
    return slice(y0, y0 + ny), slice(x0, x0 + nx)


def inner(k):
    dr, dc = DIRS[k]
    y0 = {-1: 8, 0: 8, 1: 16}[dr]
    x0 = {-1: 8, 0: 8, 1: 12}[dc]
    ny, nx = rim_rows(k)
    return slice(y0, y0 + ny), slice(x0, x0 + nx)


def pos_src(d, n):
    return {-1: slice(1, 2), 0: slice(1, n + 1), 1: slice(n, n + 1)}[d]


def pos_dst(d, n):
    return {-1: slice(n + 1, n + 2), 0: slice(1, n + 1), 1: slice(0, 1)}[d]


def main_kernel(img, w_hbm, pat, lhs, *scr):
    (wt, wv, nf, sb, rb, ext, rext, cext, tmp, hext, iext, hs) = scr[:12]
    snd_a, rcv_a, snd_b, rcv_b = scr[12:20], scr[20:28], scr[28:36], scr[36:44]
    (w_sem, a2a_send, a2a_recv, h_send, h_recv, i_send, i_recv, ca_send, ca_recv, cb_send, cb_recv) = scr[44:]
    row = lax.axis_index("row")
    col = lax.axis_index("col")
    me = row * COLS + col

    for ref in (hext, iext):
        ref[...] = jnp.zeros(ref.shape, ref.dtype)
    for ref in (*rcv_a, *rcv_b):
        ref[...] = jnp.zeros(ref.shape, ref.dtype)

    barrier = pltpu.get_barrier_semaphore()

    def greet(i, carry):
        t = lax.rem(me + i, DEVS)
        pl.semaphore_signal(
            barrier, inc=1, device_id=(lax.div(t, COLS), lax.rem(t, COLS)), device_id_type=MESH
        )
        return carry

    lax.fori_loop(1, DEVS, greet, 0)

    w_copy = pltpu.make_async_copy(w_hbm, wt, w_sem)
    w_copy.start()

    pixels = img[...].reshape(CH * WIDTH, HEIGHT).astype(F32)
    count = CH * HEIGHT * WIDTH
    center = jnp.sum(pixels, axis=(0, 1), keepdims=True) / count
    shifted = pixels - center
    variance = jnp.sum(shifted * shifted, axis=(0, 1), keepdims=True) / count
    normed = shifted / jnp.sqrt(variance + EPS)
    for c in range(CH):
        plane = normed[c * WIDTH : (c + 1) * WIDTH]
        rows = slice(c * HEIGHT, (c + 1) * HEIGHT)
        nf[0, rows, :] = plane[0:128].T
        nf[1, rows, 0:64] = plane[128:192].T
        nf[1, rows, 64:128] = jnp.zeros((HEIGHT, 64), F32)

    fold = jnp.concatenate(
        [nf[half, pl.ds(j, 96, stride=4), :] for j in range(4) for half in range(2)], axis=1
    ).astype(BF16)
    apart = lax.broadcasted_iota(jnp.int32, (128, 128), 0) - lax.broadcasted_iota(
        jnp.int32, (128, 128), 1
    )
    lane = lax.broadcasted_iota(jnp.int32, (128, 128), 1)

    def cut(t, carry):
        picks = []
        for j in range(4):
            here = (lane >= 32 * j) & (lane < 32 * j + 28)
            for half in range(2):
                hit = here & (apart == 12 * t - 8 - 32 * j - 128 * half)
                picks.append(jnp.where(hit, 1.0, 0.0).astype(BF16))
        pick = jnp.concatenate(picks, axis=0)
        block = jnp.dot(fold, pick, preferred_element_type=F32).astype(BF16)
        view = sb.at[t].reshape(CH * 64, 128)
        for c in range(CH):
            view[c * 64 : c * 64 + 16, :] = jnp.zeros((16, 128), BF16)
            view[c * 64 + 16 : c * 64 + 48, :] = block[c * 32 : c * 32 + 32]
            view[c * 64 + 48 : c * 64 + 64, :] = jnp.zeros((16, 128), BF16)
        return carry

    lax.fori_loop(0, COLS, cut, 0)

    pl.semaphore_wait(barrier, DEVS - 1)

    own = pltpu.make_async_copy(
        sb.at[col, :, pl.ds(7 + 2 * row, 4)], rb.at[:, :, me], a2a_recv
    )
    own.start()

    def send_block(i, carry):
        t = lax.rem(me + i, DEVS)
        tr = lax.div(t, COLS)
        tc = lax.rem(t, COLS)
        pltpu.make_async_remote_copy(
            src_ref=sb.at[tc, :, pl.ds(7 + 2 * tr, 4)],
            dst_ref=rb.at[:, :, me],
            send_sem=a2a_send,
            recv_sem=a2a_recv,
            device_id=(tr, tc),
            device_id_type=MESH,
        ).start()
        return carry

    lax.fori_loop(1, DEVS, send_block, 0)

    rext[...] = jnp.zeros(rext.shape, F32)
    cext[...] = jnp.zeros(cext.shape, F32)
    w_copy.wait()

    def flip(pos, carry):
        for kb in range(0, K, 128):
            n = min(128, K - kb)
            wv[pos, :, kb : kb + n] = wt[pos, kb : kb + n, :].T
        return carry

    lax.fori_loop(0, PR * PC, flip, 0)

    mr = lax.broadcasted_iota(jnp.int32, (256, 256), 0)
    mc = lax.broadcasted_iota(jnp.int32, (256, 256), 1)
    split = jnp.where(
        mr == jnp.where(mc < 128, 2 * mc, 2 * mc - 255), 1.0, 0.0
    ).astype(BF16)

    pltpu.make_async_copy(rb, rb, a2a_recv).wait()

    for c in range(CH):
        for i in range(4):
            pair = rb.at[c, i].reshape(256, 128)[...]
            turned = lax.dot_general(
                pair, split, (((0,), (0,)), ((), ())), preferred_element_type=F32
            )
            for par in range(2):
                y0 = 8 * i + 4 * par
                ext[c, y0 : y0 + 4] = turned[:, par * 128 : par * 128 + 128].reshape(4, 32, 128)

    def patch(src, base, p, q):
        for j in range(CH * FIELD):
            c, u = divmod(j, FIELD)
            tmp[pl.ds(base + FIELD * j, FIELD), :] = src[c, S * p + u, pl.ds(S * q, FIELD), :]
        return tmp[pl.ds(pl.multiple_of(base, 8), K), :].astype(BF16)

    def forward(pos, carry):
        p = lax.div(pos, PC)
        q = pos - PC * p
        base = lax.rem(pos, 2) * K
        columns = patch(ext, base, p, q)
        pat[pos, :, 0:128] = columns
        hidden = jnp.dot(wv[pos], columns, preferred_element_type=F32).astype(BF16)
        hext[p + 1, q + 1] = hidden
        terms = jnp.dot(wt[pos], hidden, preferred_element_type=F32)
        tmp[pl.ds(pl.multiple_of(base, 8), K), :] = terms
        for j in range(CH * FIELD):
            c, u = divmod(j, FIELD)
            cext[c, S * p + u, pl.ds(S * q, FIELD), :] += tmp[pl.ds(base + FIELD * j, FIELD), :]
        return carry

    lax.fori_loop(0, PR * PC, forward, 0)

    def there(k):
        dr, dc = DIRS[k]
        ok = None
        for d, at, n in ((dr, row, ROWS), (dc, col, COLS)):
            if d:
                one = at > 0 if d < 0 else at < n - 1
                ok = one if ok is None else ok & one
        return ok

    def link(k, src, dst, send, recv):
        dr, dc = DIRS[k]
        return pltpu.make_async_remote_copy(
            src_ref=src,
            dst_ref=dst,
            send_sem=send.at[k],
            recv_sem=recv.at[k],
            device_id=(row + dr, col + dc),
            device_id_type=MESH,
        )

    def halo(k, ref, send, recv):
        dr, dc = DIRS[k]
        return link(
            k,
            ref.at[pos_src(dr, PR), pos_src(dc, PC)],
            ref.at[pos_dst(dr, PR), pos_dst(dc, PC)],
            send,
            recv,
        )

    def start_all(make):
        for k in range(8):
            @pl.when(there(k))
            def _(k=k):
                make(k).start()

    def arrive_all(make):
        for k in range(8):
            @pl.when(there(k))
            def _(k=k):
                make(OPP[k]).wait_recv()

    def sent_all(make):
        for k in range(8):
            @pl.when(there(k))
            def _(k=k):
                make(k).wait_send()

    def hidden_link(k):
        return halo(k, hext, h_send, h_recv)

    def inverse_link(k):
        return halo(k, iext, i_send, i_recv)

    def contrib_link(k):
        return link(k, snd_a[k], rcv_a[k], ca_send, ca_recv)

    def resid_link(k):
        return link(k, snd_b[k], rcv_b[k], cb_send, cb_recv)

    for k in range(8):
        ys, xs = outer(k)
        snd_a[k][...] = cext[:, ys, xs, :].reshape(snd_a[k].shape).astype(BF16)
    start_all(contrib_link)
    start_all(hidden_link)

    arrive_all(hidden_link)

    def box(get, rows_out, cols_out):
        grid = [[get(a, b) for b in range(cols_out + 2)] for a in range(rows_out + 2)]
        tall = [
            [grid[a][b] + grid[a + 1][b] + grid[a + 2][b] for b in range(cols_out + 2)]
            for a in range(rows_out)
        ]
        return [
            [tall[a][b] + tall[a][b + 1] + tall[a][b + 2] for b in range(cols_out)]
            for a in range(rows_out)
        ]

    def pool(n, carry):
        rows16 = pl.ds(pl.multiple_of(n * 16, 16), 16)

        def square(a, b):
            v = hext[a, b, rows16, :].astype(F32)
            return v * v

        sums = box(square, PR, PC)
        for a in range(PR):
            for b in range(PC):
                energy = jnp.sqrt(1.0 + sums[a][b])
                iext[a + 1, b + 1, rows16, :] = (1.0 / energy).astype(BF16)
        return carry

    lax.fori_loop(0, 8, pool, 0)
    start_all(inverse_link)

    arrive_all(contrib_link)
    for k in range(8):
        ys, xs = inner(k)
        ny, nx = rim_rows(k)
        cext[:, ys, xs, :] += rcv_a[OPP[k]][...].astype(F32).reshape(CH, ny, nx, 128)
    for xs in (slice(8, 16), slice(16, 20)):
        resid = cext[:, 8:24, xs, :] - ext[:, 8:24, xs, :]
        rext[:, 8:24, xs, :] = resid.astype(BF16).astype(F32)
    for k in range(8):
        ys, xs = inner(k)
        snd_b[k][...] = rext[:, ys, xs, :].reshape(snd_b[k].shape).astype(BF16)
    start_all(resid_link)

    arrive_all(inverse_link)

    def widen(n, carry):
        rows16 = pl.ds(pl.multiple_of(n * 16, 16), 16)
        sums = box(lambda a, b: iext[a, b, rows16, :].astype(F32), PR, PC)
        for a in range(PR):
            for b in range(PC):
                hidden = hext[a + 1, b + 1, rows16, :]
                lhs[a * PC + b, rows16, 128:256] = hidden
                hs[a * PC + b, rows16, :] = SPARSITY * hidden.astype(F32) * sums[a][b]
        return carry

    lax.fori_loop(0, 8, widen, 0)

    arrive_all(resid_link)
    for k in ORDER:
        ys, xs = outer(k)
        ny, nx = rim_rows(k)
        got = rcv_b[OPP[k]][...].astype(F32).reshape(CH, ny, nx, 128)
        if nx == 16:
            rext[:, ys, 8:16, :] = got[:, :, 0:8]
            rext[:, ys, 16:20, :] = got[:, :, 8:12]
        else:
            rext[:, ys, xs, :] = got

    def backward(pos, carry):
        p = lax.div(pos, PC)
        q = pos - PC * p
        base = lax.rem(pos, 2) * K
        columns = patch(rext, base, p, q)
        pat[pos, :, 128:256] = columns
        back = hs[pos] + jnp.dot(wv[pos], columns, preferred_element_type=F32)
        lhs[pos, :, 0:128] = back.astype(BF16)
        return carry

    lax.fori_loop(0, PR * PC, backward, 0)

    pltpu.make_async_copy(
        rb.at[:, :, pl.ds(0, DEVS - 1)], rb.at[:, :, pl.ds(0, DEVS - 1)], a2a_send
    ).wait()
    for make in (hidden_link, inverse_link, contrib_link, resid_link):
        sent_all(make)


def grad_kernel(pat, lhs, out):
    pos = pl.program_id(0)
    grad = lax.dot_general(
        pat[pos], lhs[pos], (((1,), (1,)), ((), ())), preferred_element_type=F32
    )
    out[0] = grad * (1.0 / B)


def main_call(images, weights):
    rims = [CH * rim_rows(k)[0] * rim_rows(k)[1] for k in range(8)]
    bufs = [pltpu.VMEM((n, 128), BF16) for n in rims]
    dma = pltpu.SemaphoreType.DMA
    vmem = pl.BlockSpec(memory_space=pltpu.VMEM)
    n_pos = PR * PC
    return pl.pallas_call(
        main_kernel,
        name="rica_main",
        out_shape=(pltpu.VMEM((n_pos, K, 256), BF16), pltpu.VMEM((n_pos, F, 256), BF16)),
        in_specs=[vmem, pl.BlockSpec(memory_space=pltpu.HBM)],
        out_specs=(vmem, vmem),
        scratch_shapes=[
            pltpu.VMEM((n_pos, K, F), BF16),
            pltpu.VMEM((n_pos, F, K), BF16),
            pltpu.VMEM((2, CH * HEIGHT, 128), F32),
            pltpu.VMEM((COLS, CH, 32, 2, 128), BF16),
            pltpu.VMEM((CH, 4, DEVS, 2, 128), BF16),
            pltpu.VMEM((CH, 32, 32, 128), F32),
            pltpu.VMEM((CH, 32, 32, 128), F32),
            pltpu.VMEM((CH, 32, 32, 128), F32),
            pltpu.VMEM((2 * K, 128), F32),
            pltpu.VMEM((PR + 2, PC + 2, F, B), BF16),
            pltpu.VMEM((PR + 2, PC + 2, F, B), BF16),
            pltpu.VMEM((n_pos, F, B), F32),
            *bufs,
            *bufs,
            *bufs,
            *bufs,
            dma,
            dma,
            dma,
            *[dma((8,)) for _ in range(8)],
        ],
        compiler_params=pltpu.CompilerParams(
            collective_id=0, has_side_effects=True, vmem_limit_bytes=40 * 1024 * 1024
        ),
    )(images, weights)


def grad_call(pat, lhs):
    n_pos = PR * PC
    vmem = pl.BlockSpec(memory_space=pltpu.VMEM)
    return pl.pallas_call(
        grad_kernel,
        name="rica_grad",
        grid=(n_pos,),
        out_shape=jax.ShapeDtypeStruct((n_pos, K, F), F32),
        in_specs=[vmem, vmem],
        out_specs=pl.BlockSpec((1, K, F), lambda i: (i, 0, 0)),
        compiler_params=pltpu.CompilerParams(vmem_limit_bytes=12 * 1024 * 1024),
    )(pat, lhs)


def body(images, weights):
    images = images.reshape(CH, HEIGHT, WIDTH).transpose(0, 2, 1)
    weights = weights.reshape(PR * PC, F, K).transpose(0, 2, 1)
    weights = pltpu.with_memory_space_constraint(weights, pltpu.HBM)
    pat, lhs = main_call(images, weights)
    pat = pltpu.with_memory_space_constraint(pat, pltpu.VMEM)
    lhs = pltpu.with_memory_space_constraint(lhs, pltpu.VMEM)
    grad = grad_call(pat, lhs)
    return grad.transpose(0, 2, 1).reshape(PR, PC, F, K)


def solution(mesh):
    return jax.shard_map(
        body,
        mesh=mesh,
        in_specs=(P(("row", "col"), None, None, None), P("row", "col", None, None)),
        out_specs=P("row", "col", None, None),
        check_vma=False,
    )
```

profile of v0, /device:TPU:97, one launch (start us, length us, event | category | flops | bytes accessed | tf_op | source)
XLA Modules:
  0.0 74.2 jit_solution(159534153527394611)
XLA Ops:
  0.0 0.0 copy-start
  0.0 0.9 %copy-done = bf16[1,3,128,192]{2,3,1,0:T(8,128)(2,1)S(1)} copy-done((bf16[1,3,128,192]{2,3,1,0:T(8,128)(2,1)S(1)}, bf16[1,3,128,192]{2,3,1,0:T(8,128)(2,1)}, u32[]{:S(2)}) %copy-start) | copy-done | bytes 147480
  0.9 66.1 %rica_main.1 = (bf16[12,1200,256]{2,1,0:T(8,128)(2,1)S(1)}, bf16[12,128,256]{2,1,0:T(8,128)(2,1)S(1)}) custom-call(bf16[3,192,128]{2,1,0:T(8,128)(2,1)S(1)} %bitcast.9, bf16[12,1200,128]{2,1,0:T(8,128)(2,1)} %bitcast.10), custom_call_target="tpu_custom_call" | custom-call | tf_op jit(solution)/shard_map/rica_main/pallas_call | solution.py:372
  67.0 7.2 %rica_grad.1 = f32[12,1200,128]{2,1,0:T(8,128)} custom-call(bf16[12,1200,256]{2,1,0:T(8,128)(2,1)S(1)} %get-tuple-element.7.pat, bf16[12,128,256]{2,1,0:T(8,128)(2,1)S(1)} %get-tuple-element.8.lhs), custom_call_target="tpu_custom_call" | custom-call | tf_op jit(solution)/shard_map/rica_grad/pallas_call | solution.py:409
Async XLA Ops:
  0.0 0.9 %copy-start = (bf16[1,3,128,192]{2,3,1,0:T(8,128)(2,1)S(1)}, bf16[1,3,128,192]{2,3,1,0:T(8,128)(2,1)}, u32[]{:S(2)}) copy-start(bf16[1,3,128,192]{2,3,1,0:T(8,128)(2,1)} %param.2) | copy-start | bytes 442372
where the time goes:
time: 74.9 us; the launch traced here: 74.2 us
  Pallas kernels  73.3 us (98%)
  local copies, waits for them, and re-layouts  0.91 us (1%)
    pallas_call x1, Pallas kernels, main_call(): pl.pallas_call(main_kernel, name='rica_main', out_shape=(pltpu.VMEM((n_po...  66.1 us
    pallas_call x1, Pallas kernels, grad_call(): pl.pallas_call(grad_kernel, name='rica_grad', grid=(n_pos,), out_shape=ja...  7.22 us

commit v1 on v0

v1 whole, which is shorter than its diff:
```python
import jax
import jax.numpy as jnp
from jax import lax
from jax.experimental import pallas as pl
from jax.experimental.pallas import tpu as pltpu
from jax.sharding import PartitionSpec as P

MESH = pl.DeviceIdType.MESH
F32 = jnp.float32
BF16 = jnp.bfloat16

ROWS, COLS = 8, 16
DEVS = ROWS * COLS
CH, S, FIELD, PAD = 3, 4, 20, 8
K = 1200
F = 128
B = 128
HEIGHT, WIDTH = 128, 192
PR, PC = 4, 3
SPARSITY = 0.5
EPS = 1e-05

DIRS = [(dr, dc) for dr in (-1, 0, 1) for dc in (-1, 0, 1) if (dr, dc) != (0, 0)]
OPP = [DIRS.index((-dr, -dc)) for dr, dc in DIRS]
ORDER = sorted(range(8), key=lambda k: DIRS[k][1] != 0)


def rim_rows(k):
    dr, dc = DIRS[k]
    ny = 16 if dr == 0 else 8
    nx = 16 if dc == 0 else 8
    return ny, nx


def rim(d, starts, wide):
    return (8, 16) if d == 0 else (starts[d], wide)


def outer(k):
    dr, dc = DIRS[k]
    y0 = {-1: 0, 0: 8, 1: 24}[dr]
    x0 = {-1: 8, 0: 16, 1: 28}[dc]
    ny, nx = rim_rows(k)
    return slice(y0, y0 + ny), slice(x0, x0 + nx)


def inner(k):
    dr, dc = DIRS[k]
    y0 = {-1: 8, 0: 8, 1: 16}[dr]
    x0 = {-1: 16, 0: 16, 1: 20}[dc]
    ny, nx = rim_rows(k)
    return slice(y0, y0 + ny), slice(x0, x0 + nx)


def pos_src(d, n):
    return {-1: slice(1, 2), 0: slice(1, n + 1), 1: slice(n, n + 1)}[d]


def pos_dst(d, n):
    return {-1: slice(n + 1, n + 2), 0: slice(1, n + 1), 1: slice(0, 1)}[d]


def main_kernel(img_hbm, w_hbm, pat, rpat, back_out, hid_out, *scr):
    (img, wt, wv, strip, sb, rb, ext, rext, cext, hext, iext, hs) = scr[:12]
    snd_a, rcv_a, snd_b, rcv_b = scr[12:20], scr[20:28], scr[28:36], scr[36:44]
    (im_sem, w_sem, a2a_send, a2a_recv, h_send, h_recv, i_send, i_recv, ca_send, ca_recv, cb_send, cb_recv) = scr[44:]
    row = lax.axis_index("row")
    col = lax.axis_index("col")
    me = row * COLS + col

    im_copy = pltpu.make_async_copy(img_hbm, img, im_sem)
    im_copy.start()

    def there(k):
        dr, dc = DIRS[k]
        ok = None
        for d, at, n in ((dr, row, ROWS), (dc, col, COLS)):
            if d:
                one = at > 0 if d < 0 else at < n - 1
                ok = one if ok is None else ok & one
        return ok

    for k in range(8):

        @pl.when(jnp.logical_not(there(k)))
        def _(k=k):
            dr, dc = DIRS[OPP[k]]
            for ref in (hext, iext):
                for a in range(*pos_dst(dr, PR).indices(PR + 2)):
                    for b in range(*pos_dst(dc, PC).indices(PC + 2)):
                        ref[a, b] = jnp.zeros((F, B), BF16)
            for ref in (rcv_a[OPP[k]], rcv_b[OPP[k]]):
                ref[...] = jnp.zeros(ref.shape, BF16)

    barrier = pltpu.get_barrier_semaphore()

    def greet(i, carry):
        tr = (row + i) & (ROWS - 1)
        for j in range(COLS):
            pl.semaphore_signal(
                barrier, inc=1, device_id=(tr, (col + j) & (COLS - 1)), device_id_type=MESH
            )
        return carry

    lax.fori_loop(1, ROWS, greet, 0)
    for j in range(1, COLS):
        pl.semaphore_signal(
            barrier, inc=1, device_id=(row, (col + j) & (COLS - 1)), device_id_type=MESH
        )

    w_copy = pltpu.make_async_copy(w_hbm, wt, w_sem)
    w_copy.start()

    im_copy.wait()
    pixels = img[...].reshape(CH * WIDTH, HEIGHT).astype(F32)
    count = CH * HEIGHT * WIDTH
    center = jnp.sum(pixels, axis=(0, 1), keepdims=True) / count
    shifted = pixels - center
    variance = jnp.sum(shifted * shifted, axis=(0, 1), keepdims=True) / count
    normed = (shifted / jnp.sqrt(variance + EPS)).astype(BF16)

    planes = jnp.concatenate([normed[c * WIDTH : (c + 1) * WIDTH] for c in range(CH)], axis=1)
    yy = lax.broadcasted_iota(jnp.int32, (HEIGHT, 128), 0)
    lane = lax.broadcasted_iota(jnp.int32, (HEIGHT, 128), 1)
    where_from = []
    for c in range(CH):
        offset = jnp.where((lane >> 5) == c, yy - 4 * (lane & 31), -1)
        where_from.append(
            jnp.concatenate([jnp.where(offset == j, 1.0, 0.0) for j in range(4)], axis=1)
        )
    spread_y = jnp.concatenate(where_from, axis=0).astype(BF16)
    strips = jnp.dot(planes, spread_y, preferred_element_type=F32)
    for j in range(4):
        strip[j, 0:8, :] = jnp.zeros((8, 128), F32)
        strip[j, 8 : 8 + WIDTH, :] = strips[:, j * 128 : j * 128 + 128]
        strip[j, 8 + WIDTH : 32 + WIDTH, :] = jnp.zeros((24, 128), F32)

    def cut(t, carry):
        parts = [strip[j, pl.ds(12 * t, 32), :] for j in range(4)]
        block = jnp.concatenate(parts, axis=0).astype(BF16).T
        view = sb.at[t].reshape(CH * 64, 128)
        for c in range(CH):
            view[c * 64 : c * 64 + 16, :] = jnp.zeros((16, 128), BF16)
            view[c * 64 + 16 : c * 64 + 48, :] = block[c * 32 : c * 32 + 32]
            view[c * 64 + 48 : c * 64 + 64, :] = jnp.zeros((16, 128), BF16)
        return carry

    lax.fori_loop(0, COLS, cut, 0)

    pl.semaphore_wait(barrier, DEVS - 1)

    own = pltpu.make_async_copy(
        sb.at[col, :, pl.ds(7 + 2 * row, 4)], rb.at[:, :, me], a2a_recv
    )
    own.start()

    def send_block(tr, tc):
        pltpu.make_async_remote_copy(
            src_ref=sb.at[tc, :, pl.ds(7 + 2 * tr, 4)],
            dst_ref=rb.at[:, :, me],
            send_sem=a2a_send,
            recv_sem=a2a_recv,
            device_id=(tr, tc),
            device_id_type=MESH,
        ).start()

    def send_row(i, carry):
        tr = (row + i) & (ROWS - 1)
        for j in range(COLS):
            send_block(tr, (col + j) & (COLS - 1))
        return carry

    lax.fori_loop(1, ROWS, send_row, 0)
    for j in range(1, COLS):
        send_block(row, (col + j) & (COLS - 1))

    cext[...] = jnp.zeros(cext.shape, F32)
    w_copy.wait()

    def flip(pos, carry):
        for kb in range(0, K, 128):
            n = min(128, K - kb)
            wv[pos, :, kb : kb + n] = wt[pos, kb : kb + n, :].T
        return carry

    lax.fori_loop(0, PR * PC, flip, 0)

    mr = lax.broadcasted_iota(jnp.int32, (256, 256), 0)
    mc = lax.broadcasted_iota(jnp.int32, (256, 256), 1)
    split = jnp.where(
        mr == jnp.where(mc < 128, 2 * mc, 2 * mc - 255), 1.0, 0.0
    ).astype(BF16)

    pltpu.make_async_copy(rb, rb, a2a_recv).wait()

    for c in range(CH):
        for i in range(4):
            pair = rb.at[c, i].reshape(256, 128)[...]
            turned = lax.dot_general(
                pair, split, (((0,), (0,)), ((), ())), preferred_element_type=F32
            )
            for par in range(2):
                y0 = 8 * i + 4 * par
                ext[c, y0 : y0 + 4, 8:40, :] = turned[:, par * 128 : par * 128 + 128].reshape(4, 32, 128)

    low = lax.broadcasted_iota(jnp.int32, (8, 128), 0) < 4

    def patch(src, p, x0):
        blocks = []
        for c in range(CH):
            for u in range(0, FIELD, 2):
                y = S * p + u
                blocks += [
                    src[c, y, pl.ds(x0, 8), :],
                    src[c, y, pl.ds(x0 + 8, 8), :],
                    jnp.where(low, src[c, y, pl.ds(x0 + 16, 8), :], src[c, y + 1, pl.ds(x0 - 4, 8), :]),
                    src[c, y + 1, pl.ds(x0 + 4, 8), :],
                    src[c, y + 1, pl.ds(x0 + 12, 8), :],
                ]
        return jnp.concatenate(blocks, axis=0).astype(BF16)

    def unpatch(dst, terms, p, x0):
        blocks = [terms[8 * m : 8 * m + 8] for m in range(K // 8)]
        for c in range(CH):
            for u in range(0, FIELD, 2):
                y = S * p + u
                b0, b1, b2, b3, b4 = blocks[(c * FIELD + u) // 2 * 5 :][:5]
                dst[c, y, pl.ds(x0, 8), :] += b0
                dst[c, y, pl.ds(x0 + 8, 8), :] += b1
                dst[c, y, pl.ds(x0 + 16, 8), :] += jnp.where(low, b2, 0.0)
                dst[c, y + 1, pl.ds(x0 - 4, 8), :] += jnp.where(low, 0.0, b2)
                dst[c, y + 1, pl.ds(x0 + 4, 8), :] += b3
                dst[c, y + 1, pl.ds(x0 + 12, 8), :] += b4

    def encode(p, carry):
        zero = lax.shift_right_logical(p, 4)
        for q in range(PC):
            pos = PC * p + q
            columns = patch(ext, p, zero + (8 + S * q))
            pat[pos] = columns
            hidden = jnp.dot(wv[pos], columns, preferred_element_type=F32).astype(BF16)
            hext[p + 1, q + 1] = hidden
            hid_out[pos] = hidden
        return carry

    lax.fori_loop(0, PR, encode, 0)

    def link(k, src, dst, send, recv):
        dr, dc = DIRS[k]
        return pltpu.make_async_remote_copy(
            src_ref=src,
            dst_ref=dst,
            send_sem=send.at[k],
            recv_sem=recv.at[k],
            device_id=(row + dr, col + dc),
            device_id_type=MESH,
        )

    def halo(k, ref, send, recv):
        dr, dc = DIRS[k]
        return link(
            k,
            ref.at[pos_src(dr, PR), pos_src(dc, PC)],
            ref.at[pos_dst(dr, PR), pos_dst(dc, PC)],
            send,
            recv,
        )

    def start_all(make):
        for k in range(8):
            @pl.when(there(k))
            def _(k=k):
                make(k).start()

    def arrive_all(make):
        for k in range(8):
            @pl.when(there(k))
            def _(k=k):
                make(OPP[k]).wait_recv()

    def sent_all(make):
        for k in range(8):
            @pl.when(there(k))
            def _(k=k):
                make(k).wait_send()

    def hidden_link(k):
        return halo(k, hext, h_send, h_recv)

    def inverse_link(k):
        return halo(k, iext, i_send, i_recv)

    def contrib_link(k):
        return link(k, snd_a[k], rcv_a[k], ca_send, ca_recv)

    def resid_link(k):
        return link(k, snd_b[k], rcv_b[k], cb_send, cb_recv)

    start_all(hidden_link)

    def decode(p, carry):
        zero = lax.shift_right_logical(p, 4)
        for q in range(PC):
            pos = PC * p + q
            terms = jnp.dot(wt[pos], hid_out[pos], preferred_element_type=F32)
            unpatch(cext, terms, p, zero + (8 + S * q))
        return carry

    lax.fori_loop(0, PR, decode, 0)

    for k in range(8):
        ys, xs = outer(k)
        snd_a[k][...] = cext[:, ys, xs, :].reshape(snd_a[k].shape).astype(BF16)
    start_all(contrib_link)

    arrive_all(hidden_link)

    def box(get, rows_out, cols_out):
        grid = [[get(a, b) for b in range(cols_out + 2)] for a in range(rows_out + 2)]
        tall = [
            [grid[a][b] + grid[a + 1][b] + grid[a + 2][b] for b in range(cols_out + 2)]
            for a in range(rows_out)
        ]
        return [
            [tall[a][b] + tall[a][b + 1] + tall[a][b + 2] for b in range(cols_out)]
            for a in range(rows_out)
        ]

    def pool(n, carry):
        rows16 = pl.ds(pl.multiple_of(n * 16, 16), 16)

        def square(a, b):
            v = hext[a, b, rows16, :].astype(F32)
            return v * v

        sums = box(square, PR, PC)
        for a in range(PR):
            for b in range(PC):
                energy = jnp.sqrt(1.0 + sums[a][b])
                iext[a + 1, b + 1, rows16, :] = (1.0 / energy).astype(BF16)
        return carry

    lax.fori_loop(0, 8, pool, 0)
    start_all(inverse_link)

    arrive_all(contrib_link)
    for k in range(8):
        ys, xs = inner(k)
        ny, nx = rim_rows(k)
        cext[:, ys, xs, :] += rcv_a[OPP[k]][...].astype(F32).reshape(CH, ny, nx, 128)
    for xs in (slice(16, 24), slice(24, 28)):
        resid = cext[:, 8:24, xs, :] - ext[:, 8:24, xs, :]
        rext[:, 8:24, xs, :] = resid.astype(BF16).astype(F32)
    for k in range(8):
        ys, xs = inner(k)
        snd_b[k][...] = rext[:, ys, xs, :].reshape(snd_b[k].shape).astype(BF16)
    start_all(resid_link)

    arrive_all(inverse_link)

    def widen(n, carry):
        rows16 = pl.ds(pl.multiple_of(n * 16, 16), 16)
        sums = box(lambda a, b: iext[a, b, rows16, :].astype(F32), PR, PC)
        for a in range(PR):
            for b in range(PC):
                hidden = hid_out[a * PC + b, rows16, :]
                hs[a * PC + b, rows16, :] = SPARSITY * hidden.astype(F32) * sums[a][b]
        return carry

    lax.fori_loop(0, 8, widen, 0)

    arrive_all(resid_link)
    for k in ORDER:
        ys, xs = outer(k)
        ny, nx = rim_rows(k)
        got = rcv_b[OPP[k]][...].astype(F32).reshape(CH, ny, nx, 128)
        if nx == 16:
            rext[:, ys, 16:24, :] = got[:, :, 0:8]
            rext[:, ys, 24:28, :] = got[:, :, 8:12]
        else:
            rext[:, ys, xs, :] = got

    def backward(p, carry):
        zero = lax.shift_right_logical(p, 4)
        for q in range(PC):
            pos = PC * p + q
            columns = patch(rext, p, zero + (8 + S * q))
            rpat[pos] = columns
            back = hs[pos] + jnp.dot(wv[pos], columns, preferred_element_type=F32)
            back_out[pos] = back.astype(BF16)
        return carry

    lax.fori_loop(0, PR, backward, 0)

    pltpu.make_async_copy(
        rb.at[:, :, pl.ds(0, DEVS - 1)], rb.at[:, :, pl.ds(0, DEVS - 1)], a2a_send
    ).wait()
    for make in (hidden_link, inverse_link, contrib_link, resid_link):
        sent_all(make)


def grad_kernel(pat, rpat, back, hid, out, stage, sems):
    halves = (slice(0, K // 2), slice(K // 2, K))
    copies = []
    for pos in range(PR * PC):
        right = jnp.concatenate([back[pos], hid[pos]], axis=1)
        for n, rows in enumerate(halves):
            left = jnp.concatenate([pat[pos, rows, :], rpat[pos, rows, :]], axis=1)
            grad = lax.dot_general(left, right, (((1,), (1,)), ((), ())), preferred_element_type=F32)
            stage[pos, rows, :] = grad * (1.0 / B)
            copy = pltpu.make_async_copy(stage.at[pos, rows], out.at[pos, rows], sems.at[pos, n])
            copy.start()
            copies.append(copy)
    for copy in copies:
        copy.wait()


def main_call(images, weights):
    rims = [CH * rim_rows(k)[0] * rim_rows(k)[1] for k in range(8)]
    bufs = [pltpu.VMEM((n, 128), BF16) for n in rims]
    dma = pltpu.SemaphoreType.DMA
    vmem = pl.BlockSpec(memory_space=pltpu.VMEM)
    hbm = pl.BlockSpec(memory_space=pltpu.HBM)
    n_pos = PR * PC
    return pl.pallas_call(
        main_kernel,
        name="rica_main",
        out_shape=(
            pltpu.VMEM((n_pos, K, B), BF16),
            pltpu.VMEM((n_pos, K, B), BF16),
            pltpu.VMEM((n_pos, F, B), BF16),
            pltpu.VMEM((n_pos, F, B), BF16),
        ),
        in_specs=[hbm, hbm],
        out_specs=(vmem, vmem, vmem, vmem),
        scratch_shapes=[
            pltpu.VMEM((CH, WIDTH, HEIGHT), BF16),
            pltpu.VMEM((n_pos, K, F), BF16),
            pltpu.VMEM((n_pos, F, K), BF16),
            pltpu.VMEM((4, WIDTH + 32, 128), F32),
            pltpu.VMEM((COLS, CH, 32, 2, 128), BF16),
            pltpu.VMEM((CH, 4, DEVS, 2, 128), BF16),
            pltpu.VMEM((CH, 32, 40, 128), F32),
            pltpu.VMEM((CH, 32, 40, 128), F32),
            pltpu.VMEM((CH, 32, 40, 128), F32),
            pltpu.VMEM((PR + 2, PC + 2, F, B), BF16),
            pltpu.VMEM((PR + 2, PC + 2, F, B), BF16),
            pltpu.VMEM((n_pos, F, B), F32),
            *bufs,
            *bufs,
            *bufs,
            *bufs,
            *[dma for _ in range(4)],
            *[dma((8,)) for _ in range(8)],
        ],
        compiler_params=pltpu.CompilerParams(
            collective_id=0, has_side_effects=True, vmem_limit_bytes=36 * 1024 * 1024
        ),
    )(images, weights)


def grad_call(*factors):
    n_pos = PR * PC
    vmem = pl.BlockSpec(memory_space=pltpu.VMEM)
    return pl.pallas_call(
        grad_kernel,
        name="rica_grad",
        out_shape=jax.ShapeDtypeStruct((n_pos, K, F), F32),
        in_specs=[vmem] * 4,
        out_specs=pl.BlockSpec(memory_space=pltpu.HBM),
        scratch_shapes=[
            pltpu.VMEM((n_pos, K, F), F32),
            pltpu.SemaphoreType.DMA((n_pos, 2)),
        ],
        compiler_params=pltpu.CompilerParams(vmem_limit_bytes=12 * 1024 * 1024),
    )(*factors)


def body(images, weights):
    images = images.reshape(CH, HEIGHT, WIDTH).transpose(0, 2, 1)
    weights = weights.reshape(PR * PC, F, K).transpose(0, 2, 1)
    images = pltpu.with_memory_space_constraint(images, pltpu.HBM)
    weights = pltpu.with_memory_space_constraint(weights, pltpu.HBM)
    factors = main_call(images, weights)
    factors = [pltpu.with_memory_space_constraint(x, pltpu.VMEM) for x in factors]
    grad = grad_call(*factors)
    return grad.transpose(0, 2, 1).reshape(PR, PC, F, K)


def solution(mesh):
    return jax.shard_map(
        body,
        mesh=mesh,
        in_specs=(P(("row", "col"), None, None, None), P("row", "col", None, None)),
        out_specs=P("row", "col", None, None),
        check_vma=False,
    )
```

time: 74.9 us -> 59 us (0.79)
  Pallas kernels: 73.3 us -> 58.5 us
  local copies, waits for them, and re-layouts: 0.91 us -> 0 us
    pallas_call x1, Pallas kernels: 66.1 us -> 55 us  [main_call(): pl.pallas_call(main_kernel, name='rica_main', out_shape=(pltpu.VMEM((n_po...]
    pallas_call x1, Pallas kernels: 7.22 us -> 3.5 us  [grad_call(): pl.pallas_call(grad_kernel, name='rica_grad', out_shape=jax.ShapeDtypeStr...]
    unnamed x2 -> x0, local copies, waits for them, and re-layouts: 0.91 us -> none
where the time goes in v1:
time: 59 us; the launch traced here: 58.5 us
  Pallas kernels  58.5 us (99%)
    pallas_call x1, Pallas kernels, main_call(): pl.pallas_call(main_kernel, name='rica_main', out_shape=(pltpu.VMEM((n_po...  55 us
    pallas_call x1, Pallas kernels, grad_call(): pl.pallas_call(grad_kernel, name='rica_grad', out_shape=jax.ShapeDtypeStr...  3.5 us

profile of v1, /device:TPU:97, one launch (start us, length us, event | category | flops | bytes accessed | tf_op | source)
XLA Modules:
  0.0 58.5 jit_solution(10270046177414704943)
XLA Ops:
  0.0 55.0 %rica_main.1 = (bf16[12,1200,128]{2,1,0:T(8,128)(2,1)S(1)}, bf16[12,1200,128]{2,1,0:T(8,128)(2,1)S(1)}, bf16[12,128,128]{2,1,0:T(8,128)(2,1)S(1)}, bf16[12,128,128]{2,1,0:T(8,128)(2,1)S(1)}) custom-call(bf16[3,192,128]{2,1,0:T(8,128)(2,1)} %bitcast.10, bf16[12,1200,128]{2,1,0:T(8,128)(2,1)} %bitcast.9), custom_call_target="tpu_custom_call" | custom-call | tf_op jit(solution)/shard_map/rica_main/pallas_call | solution.py:425
  55.0 3.5 %rica_grad.1 = f32[12,1200,128]{2,1,0:T(8,128)} custom-call(bf16[12,1200,128]{2,1,0:T(8,128)(2,1)S(1)} %get-tuple-element.9.pat, bf16[12,1200,128]{2,1,0:T(8,128)(2,1)S(1)} %get-tuple-element.10.rpat, bf16[12,128,128]{2,1,0:T(8,128)(2,1)S(1)} %get-tuple-element.11.back, bf16[12,128,128]{2,1,0:T(8,128)(2,1)S(1)} %get-tuple-element.12.hid), custom_call_target="tpu_custom_call" | custom-call | tf_op jit(solution)/shard_map/rica_grad/pallas_call | solution.py:465

commit v2 on v1

--- a/solution.py
+++ b/solution.py
@@ -20,50 +20,18 @@
 SPARSITY = 0.5
 EPS = 1e-05
 
-DIRS = [(dr, dc) for dr in (-1, 0, 1) for dc in (-1, 0, 1) if (dr, dc) != (0, 0)]
-OPP = [DIRS.index((-dr, -dc)) for dr, dc in DIRS]
-ORDER = sorted(range(8), key=lambda k: DIRS[k][1] != 0)
-
-
-def rim_rows(k):
-    dr, dc = DIRS[k]
-    ny = 16 if dr == 0 else 8
-    nx = 16 if dc == 0 else 8
-    return ny, nx
-
-
-def rim(d, starts, wide):
-    return (8, 16) if d == 0 else (starts[d], wide)
-
-
-def outer(k):
-    dr, dc = DIRS[k]
-    y0 = {-1: 0, 0: 8, 1: 24}[dr]
-    x0 = {-1: 8, 0: 16, 1: 28}[dc]
-    ny, nx = rim_rows(k)
-    return slice(y0, y0 + ny), slice(x0, x0 + nx)
-
-
-def inner(k):
-    dr, dc = DIRS[k]
-    y0 = {-1: 8, 0: 8, 1: 16}[dr]
-    x0 = {-1: 16, 0: 16, 1: 20}[dc]
-    ny, nx = rim_rows(k)
-    return slice(y0, y0 + ny), slice(x0, x0 + nx)
-
-
-def pos_src(d, n):
-    return {-1: slice(1, 2), 0: slice(1, n + 1), 1: slice(n, n + 1)}[d]
-
-
-def pos_dst(d, n):
-    return {-1: slice(n + 1, n + 2), 0: slice(1, n + 1), 1: slice(0, 1)}[d]
+SIDES = (0, 1)
+OUTER = (8, 28)
+INNER = (16, 20)
+TOP = (0, 24)
+EDGE = (8, 16)
 
 
 def main_kernel(img_hbm, w_hbm, pat, rpat, back_out, hid_out, *scr):
-    (img, wt, wv, strip, sb, rb, ext, rext, cext, hext, iext, hs) = scr[:12]
-    snd_a, rcv_a, snd_b, rcv_b = scr[12:20], scr[20:28], scr[28:36], scr[36:44]
-    (im_sem, w_sem, a2a_send, a2a_recv, h_send, h_recv, i_send, i_recv, ca_send, ca_recv, cb_send, cb_recv) = scr[44:]
+    (img, wt, wv, strip, sb, rb, ext, rext, cext, hext, iext, flat, hs, edge_s, edge_r, spr_s, spr_r) = scr[:17]
+    col_s, col_r, row_s, row_r, rcol_s, rcol_r, rrow_s, rrow_r = scr[17:25]
+    im_sem, w_sem, a2a_send, a2a_recv = scr[25:29]
+    sems = scr[29:]
     row = lax.axis_index("row")
     col = lax.axis_index("col")
     me = row * COLS + col
@@ -71,26 +39,9 @@
     im_copy = pltpu.make_async_copy(img_hbm, img, im_sem)
     im_copy.start()
 
-    def there(k):
-        dr, dc = DIRS[k]
-        ok = None
-        for d, at, n in ((dr, row, ROWS), (dc, col, COLS)):
-            if d:
-                one = at > 0 if d < 0 else at < n - 1
-                ok = one if ok is None else ok & one
-        return ok
-
-    for k in range(8):
-
-        @pl.when(jnp.logical_not(there(k)))
-        def _(k=k):
-            dr, dc = DIRS[OPP[k]]
-            for ref in (hext, iext):
-                for a in range(*pos_dst(dr, PR).indices(PR + 2)):
-                    for b in range(*pos_dst(dc, PC).indices(PC + 2)):
-                        ref[a, b] = jnp.zeros((F, B), BF16)
-            for ref in (rcv_a[OPP[k]], rcv_b[OPP[k]]):
-                ref[...] = jnp.zeros(ref.shape, BF16)
+    def there(axis, side):
+        at, n = (row, ROWS) if axis == "row" else (col, COLS)
+        return at < n - 1 if side else at > 0
 
     barrier = pltpu.get_barrier_semaphore()
 
@@ -174,6 +125,21 @@
     for j in range(1, COLS):
         send_block(row, (col + j) & (COLS - 1))
 
+    for side in SIDES:
+
+        @pl.when(jnp.logical_not(there("col", side)))
+        def _(side=side):
+            for p in range(PR):
+                hext[p, 4 * side] = jnp.zeros((F, B), BF16)
+                iext[p, 4 * side] = jnp.zeros((F, B), BF16)
+            for ref in (col_r, rcol_r):
+                ref[side] = jnp.zeros(ref.shape[1:], BF16)
+
+        @pl.when(jnp.logical_not(there("row", side)))
+        def _(side=side):
+            for ref in (edge_r, spr_r, row_r, rrow_r):
+                ref[side] = jnp.zeros(ref.shape[1:], BF16)
+
     cext[...] = jnp.zeros(cext.shape, F32)
     w_copy.wait()
 
@@ -239,64 +205,64 @@
             columns = patch(ext, p, zero + (8 + S * q))
             pat[pos] = columns
             hidden = jnp.dot(wv[pos], columns, preferred_element_type=F32).astype(BF16)
-            hext[p + 1, q + 1] = hidden
+            hext[p, q + 1] = hidden
             hid_out[pos] = hidden
         return carry
 
     lax.fori_loop(0, PR, encode, 0)
 
-    def link(k, src, dst, send, recv):
-        dr, dc = DIRS[k]
-        return pltpu.make_async_remote_copy(
-            src_ref=src,
-            dst_ref=dst,
-            send_sem=send.at[k],
-            recv_sem=recv.at[k],
-            device_id=(row + dr, col + dc),
-            device_id_type=MESH,
+    class Exchange:
+        def __init__(self, n, axis, src, dst):
+            self.axis, self.src, self.dst = axis, src, dst
+            self.send, self.recv = sems[2 * n], sems[2 * n + 1]
+
+        def copy(self, side):
+            step = 1 if side else -1
+            to = (row + step, col) if self.axis == "row" else (row, col + step)
+            return pltpu.make_async_remote_copy(
+                src_ref=self.src(side),
+                dst_ref=self.dst(1 - side),
+                send_sem=self.send.at[side],
+                recv_sem=self.recv.at[side],
+                device_id=to,
+                device_id_type=MESH,
+            )
+
+        def each(self, act):
+            for side in SIDES:
+
+                @pl.when(there(self.axis, side))
+                def _(side=side):
+                    act(side)
+
+        def start(self):
+            self.each(lambda side: self.copy(side).start())
+
+        def arrive(self):
+            self.each(lambda side: self.copy(1 - side).wait_recv())
+
+        def sent(self):
+            self.each(lambda side: self.copy(side).wait_send())
+
+    def side_columns(ref):
+        return (
+            lambda side: ref.at[:, 3 if side else 1],
+            lambda side: ref.at[:, 4 if side else 0],
         )
 
-    def halo(k, ref, send, recv):
-        dr, dc = DIRS[k]
-        return link(
-            k,
-            ref.at[pos_src(dr, PR), pos_src(dc, PC)],
-            ref.at[pos_dst(dr, PR), pos_dst(dc, PC)],
-            send,
-            recv,
-        )
-
-    def start_all(make):
-        for k in range(8):
-            @pl.when(there(k))
-            def _(k=k):
-                make(k).start()
-
-    def arrive_all(make):
-        for k in range(8):
-            @pl.when(there(k))
-            def _(k=k):
-                make(OPP[k]).wait_recv()
-
-    def sent_all(make):
-        for k in range(8):
-            @pl.when(there(k))
-            def _(k=k):
-                make(k).wait_send()
-
-    def hidden_link(k):
-        return halo(k, hext, h_send, h_recv)
-
-    def inverse_link(k):
-        return halo(k, iext, i_send, i_recv)
-
-    def contrib_link(k):
-        return link(k, snd_a[k], rcv_a[k], ca_send, ca_recv)
-
-    def resid_link(k):
-        return link(k, snd_b[k], rcv_b[k], cb_send, cb_recv)
-
-    start_all(hidden_link)
+    def whole(send, recv):
+        return lambda side: send.at[side], lambda side: recv.at[side]
+
+    hidden_x = Exchange(0, "col", *side_columns(hext))
+    square_x = Exchange(1, "row", *whole(edge_s, edge_r))
+    inverse_x = Exchange(2, "col", *side_columns(iext))
+    spread_x = Exchange(3, "row", *whole(spr_s, spr_r))
+    terms_cx = Exchange(4, "col", *whole(col_s, col_r))
+    terms_rx = Exchange(5, "row", *whole(row_s, row_r))
+    resid_rx = Exchange(6, "row", *whole(rrow_s, rrow_r))
+    resid_cx = Exchange(7, "col", *whole(rcol_s, rcol_r))
+
+    hidden_x.start()
 
     def decode(p, carry):
         zero = lax.shift_right_logical(p, 4)
@@ -308,77 +274,149 @@
 
     lax.fori_loop(0, PR, decode, 0)
 
-    for k in range(8):
-        ys, xs = outer(k)
-        snd_a[k][...] = cext[:, ys, xs, :].reshape(snd_a[k].shape).astype(BF16)
-    start_all(contrib_link)
-
-    arrive_all(hidden_link)
-
-    def box(get, rows_out, cols_out):
-        grid = [[get(a, b) for b in range(cols_out + 2)] for a in range(rows_out + 2)]
-        tall = [
-            [grid[a][b] + grid[a + 1][b] + grid[a + 2][b] for b in range(cols_out + 2)]
-            for a in range(rows_out)
-        ]
-        return [
-            [tall[a][b] + tall[a][b + 1] + tall[a][b + 2] for b in range(cols_out)]
-            for a in range(rows_out)
-        ]
+    zero = lax.shift_right_logical(row, 8)
+
+    def pack_rows(src, y0):
+        blocks = []
+        for c in range(CH):
+            for y in range(y0, y0 + 8, 2):
+                blocks += [
+                    src[c, y, pl.ds(zero + 16, 8), :],
+                    jnp.where(low, src[c, y, pl.ds(zero + 24, 8), :], src[c, y + 1, pl.ds(zero + 12, 8), :]),
+                    src[c, y + 1, pl.ds(zero + 20, 8), :],
+                ]
+        return jnp.concatenate(blocks, axis=0).astype(BF16)
+
+    def unpack_rows(got, y0):
+        for c in range(CH):
+            for n in range(4):
+                at = (c * 4 + n) * 24
+                yield c, y0 + 2 * n, [got[at + 8 * m : at + 8 * m + 8] for m in range(3)]
+
+    def columns_of(src, x):
+        return src[:, :, pl.ds(zero + x, 8), :].reshape(CH * 32 * 8, 128).astype(BF16)
+
+    for side in SIDES:
+        col_s[side] = columns_of(cext, OUTER[side])
+    terms_cx.start()
+
+    hidden_x.arrive()
+
+    def across(get):
+        cells = [get(b) for b in range(PC + 2)]
+        return [cells[b] + cells[b + 1] + cells[b + 2] for b in range(PC)]
+
+    def chunk(n):
+        return pl.ds(pl.multiple_of(n * 16, 16), 16)
+
+    def squares(n, carry):
+        rows16 = chunk(n)
+        for p in range(PR):
+
+            def square(b):
+                v = hext[p, b, rows16, :].astype(F32)
+                return v * v
+
+            for q, total in enumerate(across(square)):
+                flat[p, q, rows16, :] = total
+                if p == 0:
+                    edge_s[0, q, rows16, :] = total.astype(BF16)
+                if p == PR - 1:
+                    edge_s[1, q, rows16, :] = total.astype(BF16)
+        return carry
+
+    lax.fori_loop(0, F // 16, squares, 0)
+    square_x.start()
+
+    terms_cx.arrive()
+    for side in SIDES:
+        cext[:, :, pl.ds(zero + INNER[side], 8), :] += (
+            col_r[side].astype(F32).reshape(CH, 32, 8, 128)
+        )
+    for side in SIDES:
+        row_s[side] = pack_rows(cext, TOP[side])
+    terms_rx.start()
+
+    square_x.arrive()
+
+    def down(q, rows16, outside):
+        cells = [outside[0, q, rows16, :].astype(F32)]
+        cells += [flat[p, q, rows16, :] for p in range(PR)]
+        cells += [outside[1, q, rows16, :].astype(F32)]
+        return [cells[p] + cells[p + 1] + cells[p + 2] for p in range(PR)]
 
     def pool(n, carry):
-        rows16 = pl.ds(pl.multiple_of(n * 16, 16), 16)
-
-        def square(a, b):
-            v = hext[a, b, rows16, :].astype(F32)
-            return v * v
-
-        sums = box(square, PR, PC)
-        for a in range(PR):
-            for b in range(PC):
-                energy = jnp.sqrt(1.0 + sums[a][b])
-                iext[a + 1, b + 1, rows16, :] = (1.0 / energy).astype(BF16)
-        return carry
-
-    lax.fori_loop(0, 8, pool, 0)
-    start_all(inverse_link)
-
-    arrive_all(contrib_link)
-    for k in range(8):
-        ys, xs = inner(k)
-        ny, nx = rim_rows(k)
-        cext[:, ys, xs, :] += rcv_a[OPP[k]][...].astype(F32).reshape(CH, ny, nx, 128)
-    for xs in (slice(16, 24), slice(24, 28)):
-        resid = cext[:, 8:24, xs, :] - ext[:, 8:24, xs, :]
-        rext[:, 8:24, xs, :] = resid.astype(BF16).astype(F32)
-    for k in range(8):
-        ys, xs = inner(k)
-        snd_b[k][...] = rext[:, ys, xs, :].reshape(snd_b[k].shape).astype(BF16)
-    start_all(resid_link)
-
-    arrive_all(inverse_link)
+        rows16 = chunk(n)
+        for q in range(PC):
+            for p, total in enumerate(down(q, rows16, edge_r)):
+                energy = jnp.sqrt(1.0 + total)
+                iext[p, q + 1, rows16, :] = (1.0 / energy).astype(BF16)
+        return carry
+
+    lax.fori_loop(0, F // 16, pool, 0)
+    inverse_x.start()
+
+    terms_rx.arrive()
+    for side in SIDES:
+        got = row_r[side].astype(F32)
+        for c, y, (b0, b1, b2) in unpack_rows(got, EDGE[side]):
+            cext[c, y, pl.ds(zero + 16, 8), :] += b0
+            cext[c, y, pl.ds(zero + 24, 8), :] += jnp.where(low, b1, 0.0)
+            cext[c, y + 1, pl.ds(zero + 12, 8), :] += jnp.where(low, 0.0, b1)
+            cext[c, y + 1, pl.ds(zero + 20, 8), :] += b2
+    for x, n in ((16, 8), (24, 4)):
+        at = slice(x, x + n)
+        resid = cext[:, 8:24, at, :] - ext[:, 8:24, at, :]
+        rext[:, 8:24, at, :] = resid.astype(BF16).astype(F32)
+    for side in SIDES:
+        rrow_s[side] = pack_rows(rext, EDGE[side])
+    resid_rx.start()
+
+    inverse_x.arrive()
+
+    def inverses(n, carry):
+        rows16 = chunk(n)
+        for p in range(PR):
+            for q, total in enumerate(across(lambda b: iext[p, b, rows16, :].astype(F32))):
+                flat[p, q, rows16, :] = total
+                if p == 0:
+                    spr_s[0, q, rows16, :] = total.astype(BF16)
+                if p == PR - 1:
+                    spr_s[1, q, rows16, :] = total.astype(BF16)
+        return carry
+
+    lax.fori_loop(0, F // 16, inverses, 0)
+    spread_x.start()
+
+    resid_rx.arrive()
+    for side in SIDES:
+        got = rrow_r[side].astype(F32)
+        for c, y, (b0, b1, b2) in unpack_rows(got, TOP[side]):
+            rext[c, y, pl.ds(zero + 16, 8), :] = b0
+            rext[c, y, pl.ds(zero + 24, 8), :] = b1
+            rext[c, y + 1, pl.ds(zero + 12, 8), :] = b1
+            rext[c, y + 1, pl.ds(zero + 20, 8), :] = b2
+    for side in SIDES:
+        rcol_s[side] = columns_of(rext, INNER[side])
+    resid_cx.start()
+
+    spread_x.arrive()
 
     def widen(n, carry):
-        rows16 = pl.ds(pl.multiple_of(n * 16, 16), 16)
-        sums = box(lambda a, b: iext[a, b, rows16, :].astype(F32), PR, PC)
-        for a in range(PR):
-            for b in range(PC):
-                hidden = hid_out[a * PC + b, rows16, :]
-                hs[a * PC + b, rows16, :] = SPARSITY * hidden.astype(F32) * sums[a][b]
-        return carry
-
-    lax.fori_loop(0, 8, widen, 0)
-
-    arrive_all(resid_link)
-    for k in ORDER:
-        ys, xs = outer(k)
-        ny, nx = rim_rows(k)
-        got = rcv_b[OPP[k]][...].astype(F32).reshape(CH, ny, nx, 128)
-        if nx == 16:
-            rext[:, ys, 16:24, :] = got[:, :, 0:8]
-            rext[:, ys, 24:28, :] = got[:, :, 8:12]
-        else:
-            rext[:, ys, xs, :] = got
+        rows16 = chunk(n)
+        for q in range(PC):
+            for p, total in enumerate(down(q, rows16, spr_r)):
+                hidden = hid_out[p * PC + q, rows16, :].astype(F32)
+                hs[p * PC + q, rows16, :] = SPARSITY * hidden * total
+        return carry
+
+    lax.fori_loop(0, F // 16, widen, 0)
+
+    resid_cx.arrive()
+    for side in SIDES:
+        rext[:, :, pl.ds(zero + OUTER[side], 8), :] = (
+            rcol_r[side].astype(F32).reshape(CH, 32, 8, 128)
+        )
 
     def backward(p, carry):
         zero = lax.shift_right_logical(p, 4)
@@ -395,8 +433,8 @@
     pltpu.make_async_copy(
         rb.at[:, :, pl.ds(0, DEVS - 1)], rb.at[:, :, pl.ds(0, DEVS - 1)], a2a_send
     ).wait()
-    for make in (hidden_link, inverse_link, contrib_link, resid_link):
-        sent_all(make)
+    for exchange in (hidden_x, square_x, inverse_x, spread_x, terms_cx, terms_rx, resid_rx, resid_cx):
+        exchange.sent()
 
 
 def grad_kernel(pat, rpat, back, hid, out, stage, sems):
@@ -416,8 +454,6 @@
 
 
 def main_call(images, weights):
-    rims = [CH * rim_rows(k)[0] * rim_rows(k)[1] for k in range(8)]
-    bufs = [pltpu.VMEM((n, 128), BF16) for n in rims]
     dma = pltpu.SemaphoreType.DMA
     vmem = pl.BlockSpec(memory_space=pltpu.VMEM)
     hbm = pl.BlockSpec(memory_space=pltpu.HBM)
@@ -443,15 +479,17 @@
             pltpu.VMEM((CH, 32, 40, 128), F32),
             pltpu.VMEM((CH, 32, 40, 128), F32),
             pltpu.VMEM((CH, 32, 40, 128), F32),
-            pltpu.VMEM((PR + 2, PC + 2, F, B), BF16),
-            pltpu.VMEM((PR + 2, PC + 2, F, B), BF16),
+            pltpu.VMEM((PR, PC + 2, F, B), BF16),
+            pltpu.VMEM((PR, PC + 2, F, B), BF16),
+            pltpu.VMEM((PR, PC, F, B), F32),
             pltpu.VMEM((n_pos, F, B), F32),
-            *bufs,
-            *bufs,
-            *bufs,
-            *bufs,
+            *[pltpu.VMEM((2, PC, F, B), BF16) for _ in range(4)],
+            *[pltpu.VMEM((2, CH * 32 * 8, 128), BF16) for _ in range(2)],
+            *[pltpu.VMEM((2, CH * 8 * 12, 128), BF16) for _ in range(2)],
+            *[pltpu.VMEM((2, CH * 32 * 8, 128), BF16) for _ in range(2)],
+            *[pltpu.VMEM((2, CH * 8 * 12, 128), BF16) for _ in range(2)],
             *[dma for _ in range(4)],
-            *[dma((8,)) for _ in range(8)],
+            *[dma((2,)) for _ in range(16)],
         ],
         compiler_params=pltpu.CompilerParams(
             collective_id=0, has_side_effects=True, vmem_limit_bytes=36 * 1024 * 1024

time: 59 us -> 57.8 us (0.980)
  the two profiles are of different devices: /device:TPU:97 before, /device:TPU:99 now
where the time goes in v2:
time: 57.8 us; the launch traced here: 57.7 us
  Pallas kernels  57.7 us (100%)
    pallas_call x1, Pallas kernels, main_call(): pl.pallas_call(main_kernel, name='rica_main', out_shape=(pltpu.VMEM((n_po...  54.2 us
    pallas_call x1, Pallas kernels, grad_call(): pl.pallas_call(grad_kernel, name='rica_grad', out_shape=jax.ShapeDtypeStr...  3.5 us

profile of v2, /device:TPU:99, one launch (start us, length us, event | category | flops | bytes accessed | tf_op | source)
XLA Modules:
  0.0 57.7 jit_solution(16325846205494708092)
XLA Ops:
  0.0 54.2 %rica_main.1 = (bf16[12,1200,128]{2,1,0:T(8,128)(2,1)S(1)}, bf16[12,1200,128]{2,1,0:T(8,128)(2,1)S(1)}, bf16[12,128,128]{2,1,0:T(8,128)(2,1)S(1)}, bf16[12,128,128]{2,1,0:T(8,128)(2,1)S(1)}) custom-call(bf16[3,192,128]{2,1,0:T(8,128)(2,1)} %bitcast.10, bf16[12,1200,128]{2,1,0:T(8,128)(2,1)} %bitcast.9), custom_call_target="tpu_custom_call" | custom-call | tf_op jit(solution)/shard_map/rica_main/pallas_call | solution.py:461
  54.2 3.5 %rica_grad.1 = f32[12,1200,128]{2,1,0:T(8,128)} custom-call(bf16[12,1200,128]{2,1,0:T(8,128)(2,1)S(1)} %get-tuple-element.9.pat, bf16[12,1200,128]{2,1,0:T(8,128)(2,1)S(1)} %get-tuple-element.10.rpat, bf16[12,128,128]{2,1,0:T(8,128)(2,1)S(1)} %get-tuple-element.11.back, bf16[12,128,128]{2,1,0:T(8,128)(2,1)S(1)} %get-tuple-element.12.hid), custom_call_target="tpu_custom_call" | custom-call | tf_op jit(solution)/shard_map/rica_grad/pallas_call | solution.py:503

commit v3 on v2

--- a/solution.py
+++ b/solution.py
@@ -21,17 +21,37 @@
 EPS = 1e-05
 
 SIDES = (0, 1)
-OUTER = (8, 28)
-INNER = (16, 20)
-TOP = (0, 24)
-EDGE = (8, 16)
-
-
-def main_kernel(img_hbm, w_hbm, pat, rpat, back_out, hid_out, *scr):
-    (img, wt, wv, strip, sb, rb, ext, rext, cext, hext, iext, flat, hs, edge_s, edge_r, spr_s, spr_r) = scr[:17]
-    col_s, col_r, row_s, row_r, rcol_s, rcol_r, rrow_s, rrow_r = scr[17:25]
-    im_sem, w_sem, a2a_send, a2a_recv = scr[25:29]
-    sems = scr[29:]
+DIRS = [(dr, dc) for dr in (-1, 0, 1) for dc in (-1, 0, 1) if (dr, dc) != (0, 0)]
+OUTER_Y, OUTER_X = {-1: 0, 0: 8, 1: 24}, {-1: 8, 1: 28}
+INNER_Y, INNER_X = {-1: 8, 0: 8, 1: 16}, {-1: 16, 1: 20}
+RIM = [CH * (288 // CH if dc == 0 else 8 * (16 if dr == 0 else 8)) for dr, dc in DIRS]
+
+
+def low_rows():
+    return lax.broadcasted_iota(jnp.int32, (8, 128), 0) < 4
+
+
+def patch(src, p, x0):
+    low = low_rows()
+    blocks = []
+    for c in range(CH):
+        for u in range(0, FIELD, 2):
+            y = S * p + u
+            blocks += [
+                src[c, y, pl.ds(x0, 8), :],
+                src[c, y, pl.ds(x0 + 8, 8), :],
+                jnp.where(low, src[c, y, pl.ds(x0 + 16, 8), :], src[c, y + 1, pl.ds(x0 - 4, 8), :]),
+                src[c, y + 1, pl.ds(x0 + 4, 8), :],
+                src[c, y + 1, pl.ds(x0 + 12, 8), :],
+            ]
+    return jnp.concatenate(blocks, axis=0).astype(BF16)
+
+
+def main_kernel(img_hbm, w_hbm, pat, wv, rext, hs, hid_out, *scr):
+    (img, wt, strip, sb, rb, ext, cext, hext, iext, flat, edge_s, edge_r, spr_s, spr_r) = scr[:14]
+    terms_s, terms_r, resid_s, resid_r = scr[14:22], scr[22:30], scr[30:38], scr[38:46]
+    im_sem, w_sem, a2a_send, a2a_recv = scr[46:50]
+    sems = scr[50:]
     row = lax.axis_index("row")
     col = lax.axis_index("col")
     me = row * COLS + col
@@ -132,13 +152,27 @@
             for p in range(PR):
                 hext[p, 4 * side] = jnp.zeros((F, B), BF16)
                 iext[p, 4 * side] = jnp.zeros((F, B), BF16)
-            for ref in (col_r, rcol_r):
-                ref[side] = jnp.zeros(ref.shape[1:], BF16)
 
         @pl.when(jnp.logical_not(there("row", side)))
         def _(side=side):
-            for ref in (edge_r, spr_r, row_r, rrow_r):
+            for ref in (edge_r, spr_r):
                 ref[side] = jnp.zeros(ref.shape[1:], BF16)
+
+    def near(k):
+        dr, dc = DIRS[k]
+        ok = None
+        for axis, d in (("row", dr), ("col", dc)):
+            if d:
+                one = there(axis, (d + 1) // 2)
+                ok = one if ok is None else ok & one
+        return ok
+
+    for k in range(8):
+
+        @pl.when(jnp.logical_not(near(k)))
+        def _(k=k):
+            for ref in (terms_r[k], resid_r[k]):
+                ref[...] = jnp.zeros(ref.shape, BF16)
 
     cext[...] = jnp.zeros(cext.shape, F32)
     w_copy.wait()
@@ -169,21 +203,7 @@
                 y0 = 8 * i + 4 * par
                 ext[c, y0 : y0 + 4, 8:40, :] = turned[:, par * 128 : par * 128 + 128].reshape(4, 32, 128)
 
-    low = lax.broadcasted_iota(jnp.int32, (8, 128), 0) < 4
-
-    def patch(src, p, x0):
-        blocks = []
-        for c in range(CH):
-            for u in range(0, FIELD, 2):
-                y = S * p + u
-                blocks += [
-                    src[c, y, pl.ds(x0, 8), :],
-                    src[c, y, pl.ds(x0 + 8, 8), :],
-                    jnp.where(low, src[c, y, pl.ds(x0 + 16, 8), :], src[c, y + 1, pl.ds(x0 - 4, 8), :]),
-                    src[c, y + 1, pl.ds(x0 + 4, 8), :],
-                    src[c, y + 1, pl.ds(x0 + 12, 8), :],
-                ]
-        return jnp.concatenate(blocks, axis=0).astype(BF16)
+    low = low_rows()
 
     def unpatch(dst, terms, p, x0):
         blocks = [terms[8 * m : 8 * m + 8] for m in range(K // 8)]
@@ -257,10 +277,40 @@
     square_x = Exchange(1, "row", *whole(edge_s, edge_r))
     inverse_x = Exchange(2, "col", *side_columns(iext))
     spread_x = Exchange(3, "row", *whole(spr_s, spr_r))
-    terms_cx = Exchange(4, "col", *whole(col_s, col_r))
-    terms_rx = Exchange(5, "row", *whole(row_s, row_r))
-    resid_rx = Exchange(6, "row", *whole(rrow_s, rrow_r))
-    resid_cx = Exchange(7, "col", *whole(rcol_s, rcol_r))
+
+    class Around:
+        def __init__(self, n, send, recv):
+            self.bufs, self.sems = (send, recv), (sems[n], sems[n + 1])
+
+        def copy(self, k):
+            dr, dc = DIRS[k]
+            return pltpu.make_async_remote_copy(
+                src_ref=self.bufs[0][k],
+                dst_ref=self.bufs[1][7 - k],
+                send_sem=self.sems[0].at[k],
+                recv_sem=self.sems[1].at[7 - k],
+                device_id=(row + dr, col + dc),
+                device_id_type=MESH,
+            )
+
+        def each(self, act):
+            for k in range(8):
+
+                @pl.when(near(k))
+                def _(k=k):
+                    act(k)
+
+        def start(self):
+            self.each(lambda k: self.copy(k).start())
+
+        def arrive(self):
+            self.each(lambda k: self.copy(7 - k).wait_recv())
+
+        def sent(self):
+            self.each(lambda k: self.copy(k).wait_send())
+
+    terms_x = Around(8, terms_s, terms_r)
+    resid_x = Around(10, resid_s, resid_r)
 
     hidden_x.start()
 
@@ -293,12 +343,17 @@
                 at = (c * 4 + n) * 24
                 yield c, y0 + 2 * n, [got[at + 8 * m : at + 8 * m + 8] for m in range(3)]
 
-    def columns_of(src, x):
-        return src[:, :, pl.ds(zero + x, 8), :].reshape(CH * 32 * 8, 128).astype(BF16)
-
-    for side in SIDES:
-        col_s[side] = columns_of(cext, OUTER[side])
-    terms_cx.start()
+    def pack(src, k, ys, xs):
+        dr, dc = DIRS[k]
+        if dc == 0:
+            return pack_rows(src, ys[dr])
+        ny = 16 if dr == 0 else 8
+        part = src[:, ys[dr] : ys[dr] + ny, pl.ds(zero + xs[dc], 8), :]
+        return part.reshape(RIM[k], 128).astype(BF16)
+
+    for k in range(8):
+        terms_s[k][...] = pack(cext, k, OUTER_Y, OUTER_X)
+    terms_x.start()
 
     hidden_x.arrive()
 
@@ -328,15 +383,6 @@
     lax.fori_loop(0, F // 16, squares, 0)
     square_x.start()
 
-    terms_cx.arrive()
-    for side in SIDES:
-        cext[:, :, pl.ds(zero + INNER[side], 8), :] += (
-            col_r[side].astype(F32).reshape(CH, 32, 8, 128)
-        )
-    for side in SIDES:
-        row_s[side] = pack_rows(cext, TOP[side])
-    terms_rx.start()
-
     square_x.arrive()
 
     def down(q, rows16, outside):
@@ -356,21 +402,26 @@
     lax.fori_loop(0, F // 16, pool, 0)
     inverse_x.start()
 
-    terms_rx.arrive()
-    for side in SIDES:
-        got = row_r[side].astype(F32)
-        for c, y, (b0, b1, b2) in unpack_rows(got, EDGE[side]):
-            cext[c, y, pl.ds(zero + 16, 8), :] += b0
-            cext[c, y, pl.ds(zero + 24, 8), :] += jnp.where(low, b1, 0.0)
-            cext[c, y + 1, pl.ds(zero + 12, 8), :] += jnp.where(low, 0.0, b1)
-            cext[c, y + 1, pl.ds(zero + 20, 8), :] += b2
+    terms_x.arrive()
+    for k, (dr, dc) in enumerate(DIRS):
+        got = terms_r[k][...].astype(F32)
+        if dc == 0:
+            for c, y, (b0, b1, b2) in unpack_rows(got, INNER_Y[dr]):
+                cext[c, y, pl.ds(zero + 16, 8), :] += b0
+                cext[c, y, pl.ds(zero + 24, 8), :] += jnp.where(low, b1, 0.0)
+                cext[c, y + 1, pl.ds(zero + 12, 8), :] += jnp.where(low, 0.0, b1)
+                cext[c, y + 1, pl.ds(zero + 20, 8), :] += b2
+        else:
+            ny = 16 if dr == 0 else 8
+            y0 = INNER_Y[dr]
+            cext[:, y0 : y0 + ny, pl.ds(zero + INNER_X[dc], 8), :] += got.reshape(CH, ny, 8, 128)
     for x, n in ((16, 8), (24, 4)):
         at = slice(x, x + n)
         resid = cext[:, 8:24, at, :] - ext[:, 8:24, at, :]
         rext[:, 8:24, at, :] = resid.astype(BF16).astype(F32)
-    for side in SIDES:
-        rrow_s[side] = pack_rows(rext, EDGE[side])
-    resid_rx.start()
+    for k in range(8):
+        resid_s[k][...] = pack(rext, k, INNER_Y, INNER_X)
+    resid_x.start()
 
     inverse_x.arrive()
 
@@ -388,18 +439,6 @@
     lax.fori_loop(0, F // 16, inverses, 0)
     spread_x.start()
 
-    resid_rx.arrive()
-    for side in SIDES:
-        got = rrow_r[side].astype(F32)
-        for c, y, (b0, b1, b2) in unpack_rows(got, TOP[side]):
-            rext[c, y, pl.ds(zero + 16, 8), :] = b0
-            rext[c, y, pl.ds(zero + 24, 8), :] = b1
-            rext[c, y + 1, pl.ds(zero + 12, 8), :] = b1
-            rext[c, y + 1, pl.ds(zero + 20, 8), :] = b2
-    for side in SIDES:
-        rcol_s[side] = columns_of(rext, INNER[side])
-    resid_cx.start()
-
     spread_x.arrive()
 
     def widen(n, carry):
@@ -412,38 +451,39 @@
 
     lax.fori_loop(0, F // 16, widen, 0)
 
-    resid_cx.arrive()
-    for side in SIDES:
-        rext[:, :, pl.ds(zero + OUTER[side], 8), :] = (
-            rcol_r[side].astype(F32).reshape(CH, 32, 8, 128)
-        )
-
-    def backward(p, carry):
-        zero = lax.shift_right_logical(p, 4)
-        for q in range(PC):
-            pos = PC * p + q
-            columns = patch(rext, p, zero + (8 + S * q))
-            rpat[pos] = columns
-            back = hs[pos] + jnp.dot(wv[pos], columns, preferred_element_type=F32)
-            back_out[pos] = back.astype(BF16)
-        return carry
-
-    lax.fori_loop(0, PR, backward, 0)
+    resid_x.arrive()
+    for k in sorted(range(8), key=lambda k: DIRS[k][1] != 0):
+        dr, dc = DIRS[k]
+        got = resid_r[k][...].astype(F32)
+        if dc == 0:
+            for c, y, (b0, b1, b2) in unpack_rows(got, OUTER_Y[dr]):
+                rext[c, y, pl.ds(zero + 16, 8), :] = b0
+                rext[c, y, pl.ds(zero + 24, 8), :] = b1
+                rext[c, y + 1, pl.ds(zero + 12, 8), :] = b1
+                rext[c, y + 1, pl.ds(zero + 20, 8), :] = b2
+        else:
+            ny = 16 if dr == 0 else 8
+            y0 = OUTER_Y[dr]
+            rext[:, y0 : y0 + ny, pl.ds(zero + OUTER_X[dc], 8), :] = got.reshape(CH, ny, 8, 128)
 
     pltpu.make_async_copy(
         rb.at[:, :, pl.ds(0, DEVS - 1)], rb.at[:, :, pl.ds(0, DEVS - 1)], a2a_send
     ).wait()
-    for exchange in (hidden_x, square_x, inverse_x, spread_x, terms_cx, terms_rx, resid_rx, resid_cx):
+    for exchange in (hidden_x, square_x, inverse_x, spread_x, terms_x, resid_x):
         exchange.sent()
 
 
-def grad_kernel(pat, rpat, back, hid, out, stage, sems):
+def grad_kernel(pat, wv, rext, hs, hid, out, stage, sems):
     halves = (slice(0, K // 2), slice(K // 2, K))
     copies = []
+    zero = lax.shift_right_logical(lax.axis_index("row"), 8)
     for pos in range(PR * PC):
-        right = jnp.concatenate([back[pos], hid[pos]], axis=1)
+        p, q = divmod(pos, PC)
+        columns = patch(rext, p, zero + (8 + S * q))
+        back = hs[pos] + jnp.dot(wv[pos], columns, preferred_element_type=F32)
+        right = jnp.concatenate([back.astype(BF16), hid[pos]], axis=1)
         for n, rows in enumerate(halves):
-            left = jnp.concatenate([pat[pos, rows, :], rpat[pos, rows, :]], axis=1)
+            left = jnp.concatenate([pat[pos, rows, :], columns[rows]], axis=1)
             grad = lax.dot_general(left, right, (((1,), (1,)), ((), ())), preferred_element_type=F32)
             stage[pos, rows, :] = grad * (1.0 / B)
             copy = pltpu.make_async_copy(stage.at[pos, rows], out.at[pos, rows], sems.at[pos, n])
@@ -463,33 +503,29 @@
         name="rica_main",
         out_shape=(
             pltpu.VMEM((n_pos, K, B), BF16),
-            pltpu.VMEM((n_pos, K, B), BF16),
-            pltpu.VMEM((n_pos, F, B), BF16),
+            pltpu.VMEM((n_pos, F, K), BF16),
+            pltpu.VMEM((CH, 32, 40, 128), F32),
+            pltpu.VMEM((n_pos, F, B), F32),
             pltpu.VMEM((n_pos, F, B), BF16),
         ),
         in_specs=[hbm, hbm],
-        out_specs=(vmem, vmem, vmem, vmem),
+        out_specs=(vmem,) * 5,
         scratch_shapes=[
             pltpu.VMEM((CH, WIDTH, HEIGHT), BF16),
             pltpu.VMEM((n_pos, K, F), BF16),
-            pltpu.VMEM((n_pos, F, K), BF16),
             pltpu.VMEM((4, WIDTH + 32, 128), F32),
             pltpu.VMEM((COLS, CH, 32, 2, 128), BF16),
             pltpu.VMEM((CH, 4, DEVS, 2, 128), BF16),
             pltpu.VMEM((CH, 32, 40, 128), F32),
             pltpu.VMEM((CH, 32, 40, 128), F32),
-            pltpu.VMEM((CH, 32, 40, 128), F32),
             pltpu.VMEM((PR, PC + 2, F, B), BF16),
             pltpu.VMEM((PR, PC + 2, F, B), BF16),
             pltpu.VMEM((PR, PC, F, B), F32),
-            pltpu.VMEM((n_pos, F, B), F32),
             *[pltpu.VMEM((2, PC, F, B), BF16) for _ in range(4)],
-            *[pltpu.VMEM((2, CH * 32 * 8, 128), BF16) for _ in range(2)],
-            *[pltpu.VMEM((2, CH * 8 * 12, 128), BF16) for _ in range(2)],
-            *[pltpu.VMEM((2, CH * 32 * 8, 128), BF16) for _ in range(2)],
-            *[pltpu.VMEM((2, CH * 8 * 12, 128), BF16) for _ in range(2)],
+            *[pltpu.VMEM((n, 128), BF16) for _ in range(4) for n in RIM],
             *[dma for _ in range(4)],
-            *[dma((2,)) for _ in range(16)],
+            *[dma((2,)) for _ in range(8)],
+            *[dma((8,)) for _ in range(4)],
         ],
         compiler_params=pltpu.CompilerParams(
             collective_id=0, has_side_effects=True, vmem_limit_bytes=36 * 1024 * 1024
@@ -504,7 +540,7 @@
         grad_kernel,
         name="rica_grad",
         out_shape=jax.ShapeDtypeStruct((n_pos, K, F), F32),
-        in_specs=[vmem] * 4,
+        in_specs=[vmem] * 5,
         out_specs=pl.BlockSpec(memory_space=pltpu.HBM),
         scratch_shapes=[
             pltpu.VMEM((n_pos, K, F), F32),

time: 57.8 us -> 58.8 us (1.017)
  the two profiles are of different devices: /device:TPU:99 before, /device:TPU:97 now
where the time goes in v3:
time: 58.8 us; the launch traced here: 58.7 us
  Pallas kernels  58.7 us (100%)
    pallas_call x1, Pallas kernels, main_call(): pl.pallas_call(main_kernel, name='rica_main', out_shape=(pltpu.VMEM((n_po...  52.7 us
    pallas_call x1, Pallas kernels, grad_call(): pl.pallas_call(grad_kernel, name='rica_grad', out_shape=jax.ShapeDtypeStr...  6 us

profile of v3, /device:TPU:97, one launch (start us, length us, event | category | flops | bytes accessed | tf_op | source)
XLA Modules:
  0.0 58.7 jit_solution(9598104572535901441)
XLA Ops:
  0.0 52.7 %rica_main.1 = (bf16[12,1200,128]{2,1,0:T(8,128)(2,1)S(1)}, bf16[12,128,1200]{2,1,0:T(8,128)(2,1)S(1)}, f32[3,32,40,128]{3,2,1,0:T(8,128)S(1)}, f32[12,128,128]{2,1,0:T(8,128)S(1)}, bf16[12,128,128]{2,1,0:T(8,128)(2,1)S(1)}) custom-call(bf16[3,192,128]{2,1,0:T(8,128)(2,1)} %bitcast.10, bf16[12,1200,128]{2,1,0:T(8,128)(2,1)} %bitcast.9), custom_call_target="tpu_custom_call" | custom-call | tf_op jit(solution)/shard_map/rica_main/pallas_call | solution.py:501
  52.7 6.0 %rica_grad.1 = f32[12,1200,128]{2,1,0:T(8,128)} custom-call(bf16[12,1200,128]{2,1,0:T(8,128)(2,1)S(1)} %get-tuple-element.10.pat, bf16[12,128,1200]{2,1,0:T(8,128)(2,1)S(1)} %get-tuple-element.11.wv, f32[3,32,40,128]{3,2,1,0:T(8,128)S(1)} %get-tuple-element.12.rext, f32[12,128,128]{2,1,0:T(8,128)S(1)} %get-tuple-element.13.hs, ...), custom_call_target="tpu_custom_call" | custom-call | tf_op jit(solution)/shard_map/rica_grad/pallas_call | solution.py:539

commit v4 on v3

--- a/solution.py
+++ b/solution.py
@@ -31,10 +31,10 @@
     return lax.broadcasted_iota(jnp.int32, (8, 128), 0) < 4
 
 
-def patch(src, p, x0):
+def patch(src, p, x0, channels=range(CH)):
     low = low_rows()
     blocks = []
-    for c in range(CH):
+    for c in channels:
         for u in range(0, FIELD, 2):
             y = S * p + u
             blocks += [
@@ -47,11 +47,11 @@
     return jnp.concatenate(blocks, axis=0).astype(BF16)
 
 
-def main_kernel(img_hbm, w_hbm, pat, wv, rext, hs, hid_out, *scr):
-    (img, wt, strip, sb, rb, ext, cext, hext, iext, flat, edge_s, edge_r, spr_s, spr_r) = scr[:14]
-    terms_s, terms_r, resid_s, resid_r = scr[14:22], scr[22:30], scr[30:38], scr[38:46]
-    im_sem, w_sem, a2a_send, a2a_recv = scr[46:50]
-    sems = scr[50:]
+def main_kernel(img_hbm, w_hbm, pat, rpat, back_out, hid_out, *scr):
+    (wv, rext, hs, img, wt, strip, sb, rb, ext, cext, hext, iext, flat, edge_s, edge_r, spr_s, spr_r) = scr[:17]
+    terms_s, terms_r, resid_s, resid_r = scr[17:25], scr[25:33], scr[33:41], scr[41:49]
+    im_sem, w_sem, a2a_send, a2a_recv = scr[49:53]
+    sems = scr[53:]
     row = lax.axis_index("row")
     col = lax.axis_index("col")
     me = row * COLS + col
@@ -120,30 +120,30 @@
 
     pl.semaphore_wait(barrier, DEVS - 1)
 
-    own = pltpu.make_async_copy(
-        sb.at[col, :, pl.ds(7 + 2 * row, 4)], rb.at[:, :, me], a2a_recv
-    )
-    own.start()
-
-    def send_block(tr, tc):
+    def send_block(c, tr, tc):
         pltpu.make_async_remote_copy(
-            src_ref=sb.at[tc, :, pl.ds(7 + 2 * tr, 4)],
-            dst_ref=rb.at[:, :, me],
+            src_ref=sb.at[tc, c, pl.ds(7 + 2 * tr, 4)],
+            dst_ref=rb.at[c, :, me],
             send_sem=a2a_send,
-            recv_sem=a2a_recv,
+            recv_sem=a2a_recv.at[c],
             device_id=(tr, tc),
             device_id_type=MESH,
         ).start()
 
-    def send_row(i, carry):
-        tr = (row + i) & (ROWS - 1)
-        for j in range(COLS):
-            send_block(tr, (col + j) & (COLS - 1))
-        return carry
-
-    lax.fori_loop(1, ROWS, send_row, 0)
-    for j in range(1, COLS):
-        send_block(row, (col + j) & (COLS - 1))
+    for c in range(CH):
+        pltpu.make_async_copy(
+            sb.at[col, c, pl.ds(7 + 2 * row, 4)], rb.at[c, :, me], a2a_recv.at[c]
+        ).start()
+
+        def send_row(i, carry, c=c):
+            tr = (row + i) & (ROWS - 1)
+            for j in range(COLS):
+                send_block(c, tr, (col + j) & (COLS - 1))
+            return carry
+
+        lax.fori_loop(1, ROWS, send_row, 0)
+        for j in range(1, COLS):
+            send_block(c, row, (col + j) & (COLS - 1))
 
     for side in SIDES:
 
@@ -190,18 +190,6 @@
     split = jnp.where(
         mr == jnp.where(mc < 128, 2 * mc, 2 * mc - 255), 1.0, 0.0
     ).astype(BF16)
-
-    pltpu.make_async_copy(rb, rb, a2a_recv).wait()
-
-    for c in range(CH):
-        for i in range(4):
-            pair = rb.at[c, i].reshape(256, 128)[...]
-            turned = lax.dot_general(
-                pair, split, (((0,), (0,)), ((), ())), preferred_element_type=F32
-            )
-            for par in range(2):
-                y0 = 8 * i + 4 * par
-                ext[c, y0 : y0 + 4, 8:40, :] = turned[:, par * 128 : par * 128 + 128].reshape(4, 32, 128)
 
     low = low_rows()
 
@@ -218,18 +206,40 @@
                 dst[c, y + 1, pl.ds(x0 + 4, 8), :] += b3
                 dst[c, y + 1, pl.ds(x0 + 12, 8), :] += b4
 
-    def encode(p, carry):
-        zero = lax.shift_right_logical(p, 4)
-        for q in range(PC):
-            pos = PC * p + q
-            columns = patch(ext, p, zero + (8 + S * q))
-            pat[pos] = columns
-            hidden = jnp.dot(wv[pos], columns, preferred_element_type=F32).astype(BF16)
-            hext[p, q + 1] = hidden
-            hid_out[pos] = hidden
-        return carry
-
-    lax.fori_loop(0, PR, encode, 0)
+    for c in range(CH):
+        pltpu.make_async_copy(rb.at[c], rb.at[c], a2a_recv.at[c]).wait()
+        for i in range(4):
+            pair = rb.at[c, i].reshape(256, 128)[...]
+            turned = lax.dot_general(
+                pair, split, (((0,), (0,)), ((), ())), preferred_element_type=F32
+            )
+            for par in range(2):
+                y0 = 8 * i + 4 * par
+                part = turned[:, par * 128 : par * 128 + 128].reshape(4, 32, 128)
+                ext[c, y0 : y0 + 4, 8:40, :] = part
+        lo = 384 * c
+        hi = 384 * (c + 1) if c < CH - 1 else K
+
+        def encode(p, carry, c=c, lo=lo, hi=hi):
+            zero = lax.shift_right_logical(p, 4)
+            for q in range(PC):
+                pos = PC * p + q
+                columns = patch(ext, p, zero + (8 + S * q), [c])
+                pat[pos, 400 * c : 400 * c + 400, :] = columns
+                if lo < 400 * c:
+                    columns = jnp.concatenate([pat[pos, lo : 400 * c, :], columns], axis=0)
+                sums = jnp.dot(wv[pos, :, lo:hi], columns[: hi - lo], preferred_element_type=F32)
+                if c > 0:
+                    sums = sums + hs[pos]
+                if c < CH - 1:
+                    hs[pos] = sums
+                else:
+                    hidden = sums.astype(BF16)
+                    hext[p, q + 1] = hidden
+                    hid_out[pos] = hidden
+            return carry
+
+        lax.fori_loop(0, PR, encode, 0)
 
     class Exchange:
         def __init__(self, n, axis, src, dst):
@@ -439,18 +449,6 @@
     lax.fori_loop(0, F // 16, inverses, 0)
     spread_x.start()
 
-    spread_x.arrive()
-
-    def widen(n, carry):
-        rows16 = chunk(n)
-        for q in range(PC):
-            for p, total in enumerate(down(q, rows16, spr_r)):
-                hidden = hid_out[p * PC + q, rows16, :].astype(F32)
-                hs[p * PC + q, rows16, :] = SPARSITY * hidden * total
-        return carry
-
-    lax.fori_loop(0, F // 16, widen, 0)
-
     resid_x.arrive()
     for k in sorted(range(8), key=lambda k: DIRS[k][1] != 0):
         dr, dc = DIRS[k]
@@ -466,6 +464,30 @@
             y0 = OUTER_Y[dr]
             rext[:, y0 : y0 + ny, pl.ds(zero + OUTER_X[dc], 8), :] = got.reshape(CH, ny, 8, 128)
 
+    def backward(p, carry):
+        zero = lax.shift_right_logical(p, 4)
+        for q in range(PC):
+            pos = PC * p + q
+            columns = patch(rext, p, zero + (8 + S * q))
+            rpat[pos] = columns
+            hs[pos] = jnp.dot(wv[pos], columns, preferred_element_type=F32)
+        return carry
+
+    lax.fori_loop(0, PR, backward, 0)
+
+    spread_x.arrive()
+
+    def widen(n, carry):
+        rows16 = chunk(n)
+        for q in range(PC):
+            for p, total in enumerate(down(q, rows16, spr_r)):
+                hidden = hid_out[p * PC + q, rows16, :].astype(F32)
+                back = SPARSITY * hidden * total + hs[p * PC + q, rows16, :]
+                back_out[p * PC + q, rows16, :] = back.astype(BF16)
+        return carry
+
+    lax.fori_loop(0, F // 16, widen, 0)
+
     pltpu.make_async_copy(
         rb.at[:, :, pl.ds(0, DEVS - 1)], rb.at[:, :, pl.ds(0, DEVS - 1)], a2a_send
     ).wait()
@@ -473,17 +495,13 @@
         exchange.sent()
 
 
-def grad_kernel(pat, wv, rext, hs, hid, out, stage, sems):
+def grad_kernel(pat, rpat, back, hid, out, stage, sems):
     halves = (slice(0, K // 2), slice(K // 2, K))
     copies = []
-    zero = lax.shift_right_logical(lax.axis_index("row"), 8)
     for pos in range(PR * PC):
-        p, q = divmod(pos, PC)
-        columns = patch(rext, p, zero + (8 + S * q))
-        back = hs[pos] + jnp.dot(wv[pos], columns, preferred_element_type=F32)
-        right = jnp.concatenate([back.astype(BF16), hid[pos]], axis=1)
+        right = jnp.concatenate([back[pos], hid[pos]], axis=1)
         for n, rows in enumerate(halves):
-            left = jnp.concatenate([pat[pos, rows, :], columns[rows]], axis=1)
+            left = jnp.concatenate([pat[pos, rows, :], rpat[pos, rows, :]], axis=1)
             grad = lax.dot_general(left, right, (((1,), (1,)), ((), ())), preferred_element_type=F32)
             stage[pos, rows, :] = grad * (1.0 / B)
             copy = pltpu.make_async_copy(stage.at[pos, rows], out.at[pos, rows], sems.at[pos, n])
@@ -503,14 +521,16 @@
         name="rica_main",
         out_shape=(
             pltpu.VMEM((n_pos, K, B), BF16),
+            pltpu.VMEM((n_pos, K, B), BF16),
+            pltpu.VMEM((n_pos, F, B), BF16),
+            pltpu.VMEM((n_pos, F, B), BF16),
+        ),
+        in_specs=[hbm, hbm],
+        out_specs=(vmem,) * 4,
+        scratch_shapes=[
             pltpu.VMEM((n_pos, F, K), BF16),
             pltpu.VMEM((CH, 32, 40, 128), F32),
             pltpu.VMEM((n_pos, F, B), F32),
-            pltpu.VMEM((n_pos, F, B), BF16),
-        ),
-        in_specs=[hbm, hbm],
-        out_specs=(vmem,) * 5,
-        scratch_shapes=[
             pltpu.VMEM((CH, WIDTH, HEIGHT), BF16),
             pltpu.VMEM((n_pos, K, F), BF16),
             pltpu.VMEM((4, WIDTH + 32, 128), F32),
@@ -523,7 +543,8 @@
             pltpu.VMEM((PR, PC, F, B), F32),
             *[pltpu.VMEM((2, PC, F, B), BF16) for _ in range(4)],
             *[pltpu.VMEM((n, 128), BF16) for _ in range(4) for n in RIM],
-            *[dma for _ in range(4)],
+            *[dma for _ in range(3)],
+            dma((CH,)),
             *[dma((2,)) for _ in range(8)],
             *[dma((8,)) for _ in range(4)],
         ],
@@ -540,7 +561,7 @@
         grad_kernel,
         name="rica_grad",
         out_shape=jax.ShapeDtypeStruct((n_pos, K, F), F32),
-        in_specs=[vmem] * 5,
+        in_specs=[vmem] * 4,
         out_specs=pl.BlockSpec(memory_space=pltpu.HBM),
         scratch_shapes=[
             pltpu.VMEM((n_pos, K, F), F32),

time: 58.8 us -> 55.3 us (0.940)
  Pallas kernels: 58.7 us -> 54.6 us
    pallas_call x1, Pallas kernels: 6 us -> 3.5 us  [grad_call(): pl.pallas_call(grad_kernel, name='rica_grad', out_shape=jax.ShapeDtypeStr...]
    pallas_call x1, Pallas kernels: 52.7 us -> 51.1 us  [main_call(): pl.pallas_call(main_kernel, name='rica_main', out_shape=(pltpu.VMEM((n_po...]
where the time goes in v4:
time: 55.3 us; the launch traced here: 54.7 us
  Pallas kernels  54.6 us (99%)
    pallas_call x1, Pallas kernels, main_call(): pl.pallas_call(main_kernel, name='rica_main', out_shape=(pltpu.VMEM((n_po...  51.1 us
    pallas_call x1, Pallas kernels, grad_call(): pl.pallas_call(grad_kernel, name='rica_grad', out_shape=jax.ShapeDtypeStr...  3.5 us

profile of v4, /device:TPU:97, one launch (start us, length us, event | category | flops | bytes accessed | tf_op | source)
XLA Modules:
  0.0 54.7 jit_solution(6432707027226720555)
XLA Ops:
  0.0 51.1 %rica_main.1 = (bf16[12,1200,128]{2,1,0:T(8,128)(2,1)S(1)}, bf16[12,1200,128]{2,1,0:T(8,128)(2,1)S(1)}, bf16[12,128,128]{2,1,0:T(8,128)(2,1)S(1)}, bf16[12,128,128]{2,1,0:T(8,128)(2,1)S(1)}) custom-call(bf16[3,192,128]{2,1,0:T(8,128)(2,1)} %bitcast.10, bf16[12,1200,128]{2,1,0:T(8,128)(2,1)} %bitcast.9), custom_call_target="tpu_custom_call" | custom-call | tf_op jit(solution)/shard_map/rica_main/pallas_call | solution.py:519
  51.2 3.5 %rica_grad.1 = f32[12,1200,128]{2,1,0:T(8,128)} custom-call(bf16[12,1200,128]{2,1,0:T(8,128)(2,1)S(1)} %get-tuple-element.9.pat, bf16[12,1200,128]{2,1,0:T(8,128)(2,1)S(1)} %get-tuple-element.10.rpat, bf16[12,128,128]{2,1,0:T(8,128)(2,1)S(1)} %get-tuple-element.11.back, bf16[12,128,128]{2,1,0:T(8,128)(2,1)S(1)} %get-tuple-element.12.hid), custom_call_target="tpu_custom_call" | custom-call | tf_op jit(solution)/shard_map/rica_grad/pallas_call | solution.py:560

commit v5 on v4

--- a/solution.py
+++ b/solution.py
@@ -50,8 +50,9 @@
 def main_kernel(img_hbm, w_hbm, pat, rpat, back_out, hid_out, *scr):
     (wv, rext, hs, img, wt, strip, sb, rb, ext, cext, hext, iext, flat, edge_s, edge_r, spr_s, spr_r) = scr[:17]
     terms_s, terms_r, resid_s, resid_r = scr[17:25], scr[25:33], scr[33:41], scr[41:49]
-    im_sem, w_sem, a2a_send, a2a_recv = scr[49:53]
-    sems = scr[53:]
+    terms_t, resid_t = scr[49:51], scr[51:53]
+    im_sem, w_sem, a2a_send, a2a_recv = scr[53:57]
+    sems = scr[57:]
     row = lax.axis_index("row")
     col = lax.axis_index("col")
     me = row * COLS + col
@@ -288,9 +289,16 @@
     inverse_x = Exchange(2, "col", *side_columns(iext))
     spread_x = Exchange(3, "row", *whole(spr_s, spr_r))
 
+    half = ROWS // 2
+
+    def crosses(k):
+        dr, dc = DIRS[k]
+        return row == (half - 1 if dr > 0 else half) if dr and dc else None
+
     class Around:
-        def __init__(self, n, send, recv):
-            self.bufs, self.sems = (send, recv), (sems[n], sems[n + 1])
+        def __init__(self, n, send, recv, through):
+            self.bufs, self.sems = (send, recv), sems[n : n + 4]
+            self.through = through
 
         def copy(self, k):
             dr, dc = DIRS[k]
@@ -303,6 +311,28 @@
                 device_id_type=MESH,
             )
 
+        def to_relay(self, k):
+            dr, dc = DIRS[k]
+            return pltpu.make_async_remote_copy(
+                src_ref=self.bufs[0][k],
+                dst_ref=self.through[(dc + 1) // 2],
+                send_sem=self.sems[0].at[k],
+                recv_sem=self.sems[2].at[(dc + 1) // 2],
+                device_id=(row - 3 * dr, col),
+                device_id_type=MESH,
+            )
+
+        def from_relay(self, k):
+            dr, dc = DIRS[k]
+            return pltpu.make_async_remote_copy(
+                src_ref=self.through[(dc + 1) // 2],
+                dst_ref=self.bufs[1][7 - k],
+                send_sem=self.sems[3].at[(dc + 1) // 2],
+                recv_sem=self.sems[1].at[7 - k],
+                device_id=(row + half * dr, col + dc),
+                device_id_type=MESH,
+            )
+
         def each(self, act):
             for k in range(8):
 
@@ -311,16 +341,50 @@
                     act(k)
 
         def start(self):
-            self.each(lambda k: self.copy(k).start())
+            for k in range(8):
+                apart = crosses(k)
+                if apart is None:
+
+                    @pl.when(near(k))
+                    def _(k=k):
+                        self.copy(k).start()
+
+                else:
+
+                    @pl.when(near(k) & apart)
+                    def _(k=k):
+                        self.to_relay(k).start()
+
+                    @pl.when(near(k) & jnp.logical_not(apart))
+                    def _(k=k):
+                        self.copy(k).start()
+
+        def relays(self, act):
+            for k, (dr, dc) in enumerate(DIRS):
+                if dr and dc:
+
+                    @pl.when((row == (0 if dr > 0 else ROWS - 1)) & there("col", (dc + 1) // 2))
+                    def _(k=k):
+                        act(k)
+
+        def relay(self):
+            def pass_on(k):
+                slot = (DIRS[k][1] + 1) // 2
+                held = self.through[slot]
+                pltpu.make_async_copy(held, held, self.sems[2].at[slot]).wait()
+                self.from_relay(k).start()
+
+            self.relays(pass_on)
 
         def arrive(self):
             self.each(lambda k: self.copy(7 - k).wait_recv())
 
         def sent(self):
             self.each(lambda k: self.copy(k).wait_send())
-
-    terms_x = Around(8, terms_s, terms_r)
-    resid_x = Around(10, resid_s, resid_r)
+            self.relays(lambda k: self.from_relay(k).wait_send())
+
+    terms_x = Around(8, terms_s, terms_r, terms_t)
+    resid_x = Around(12, resid_s, resid_r, resid_t)
 
     hidden_x.start()
 
@@ -392,6 +456,7 @@
 
     lax.fori_loop(0, F // 16, squares, 0)
     square_x.start()
+    terms_x.relay()
 
     square_x.arrive()
 
@@ -448,6 +513,7 @@
 
     lax.fori_loop(0, F // 16, inverses, 0)
     spread_x.start()
+    resid_x.relay()
 
     resid_x.arrive()
     for k in sorted(range(8), key=lambda k: DIRS[k][1] != 0):
@@ -543,10 +609,11 @@
             pltpu.VMEM((PR, PC, F, B), F32),
             *[pltpu.VMEM((2, PC, F, B), BF16) for _ in range(4)],
             *[pltpu.VMEM((n, 128), BF16) for _ in range(4) for n in RIM],
+            *[pltpu.VMEM((RIM[0], 128), BF16) for _ in range(4)],
             *[dma for _ in range(3)],
             dma((CH,)),
             *[dma((2,)) for _ in range(8)],
-            *[dma((8,)) for _ in range(4)],
+            *[dma((n,)) for _ in range(2) for n in (8, 8, 2, 2)],
         ],
         compiler_params=pltpu.CompilerParams(
             collective_id=0, has_side_effects=True, vmem_limit_bytes=36 * 1024 * 1024

time: 55.3 us -> 53.2 us (0.962)
  Pallas kernels: 54.6 us -> 52.7 us
    pallas_call x1, Pallas kernels: 51.1 us -> 49.1 us  [main_call(): pl.pallas_call(main_kernel, name='rica_main', out_shape=(pltpu.VMEM((n_po...]
where the time goes in v5:
time: 53.2 us; the launch traced here: 52.7 us
  Pallas kernels  52.7 us (99%)
    pallas_call x1, Pallas kernels, main_call(): pl.pallas_call(main_kernel, name='rica_main', out_shape=(pltpu.VMEM((n_po...  49.1 us
    pallas_call x1, Pallas kernels, grad_call(): pl.pallas_call(grad_kernel, name='rica_grad', out_shape=jax.ShapeDtypeStr...  3.51 us

profile of v5, /device:TPU:97, one launch (start us, length us, event | category | flops | bytes accessed | tf_op | source)
XLA Modules:
  0.0 52.7 jit_solution(5045721644912013472)
XLA Ops:
  0.0 49.1 %rica_main.1 = (bf16[12,1200,128]{2,1,0:T(8,128)(2,1)S(1)}, bf16[12,1200,128]{2,1,0:T(8,128)(2,1)S(1)}, bf16[12,128,128]{2,1,0:T(8,128)(2,1)S(1)}, bf16[12,128,128]{2,1,0:T(8,128)(2,1)S(1)}) custom-call(bf16[3,192,128]{2,1,0:T(8,128)(2,1)} %bitcast.10, bf16[12,1200,128]{2,1,0:T(8,128)(2,1)} %bitcast.9), custom_call_target="tpu_custom_call" | custom-call | tf_op jit(solution)/shard_map/rica_main/pallas_call | solution.py:585
  49.2 3.5 %rica_grad.1 = f32[12,1200,128]{2,1,0:T(8,128)} custom-call(bf16[12,1200,128]{2,1,0:T(8,128)(2,1)S(1)} %get-tuple-element.9.pat, bf16[12,1200,128]{2,1,0:T(8,128)(2,1)S(1)} %get-tuple-element.10.rpat, bf16[12,128,128]{2,1,0:T(8,128)(2,1)S(1)} %get-tuple-element.11.back, bf16[12,128,128]{2,1,0:T(8,128)(2,1)S(1)} %get-tuple-element.12.hid), custom_call_target="tpu_custom_call" | custom-call | tf_op jit(solution)/shard_map/rica_grad/pallas_call | solution.py:627

commit v6 on v5

--- a/solution.py
+++ b/solution.py
@@ -74,7 +74,8 @@
             )
         return carry
 
-    lax.fori_loop(1, ROWS, greet, 0)
+    lax.fori_loop(2, ROWS, greet, 0)
+    greet(1, 0)
     for j in range(1, COLS):
         pl.semaphore_signal(
             barrier, inc=1, device_id=(row, (col + j) & (COLS - 1)), device_id_type=MESH
@@ -142,7 +143,8 @@
                 send_block(c, tr, (col + j) & (COLS - 1))
             return carry
 
-        lax.fori_loop(1, ROWS, send_row, 0)
+        lax.fori_loop(2, ROWS, send_row, 0)
+        send_row(1, 0)
         for j in range(1, COLS):
             send_block(c, row, (col + j) & (COLS - 1))
 
@@ -340,8 +342,8 @@
                 def _(k=k):
                     act(k)
 
-        def start(self):
-            for k in range(8):
+        def start(self, which=range(8)):
+            for k in which:
                 apart = crosses(k)
                 if apart is None:
 
@@ -387,16 +389,6 @@
     resid_x = Around(12, resid_s, resid_r, resid_t)
 
     hidden_x.start()
-
-    def decode(p, carry):
-        zero = lax.shift_right_logical(p, 4)
-        for q in range(PC):
-            pos = PC * p + q
-            terms = jnp.dot(wt[pos], hid_out[pos], preferred_element_type=F32)
-            unpatch(cext, terms, p, zero + (8 + S * q))
-        return carry
-
-    lax.fori_loop(0, PR, decode, 0)
 
     zero = lax.shift_right_logical(row, 8)
 
@@ -425,9 +417,23 @@
         part = src[:, ys[dr] : ys[dr] + ny, pl.ds(zero + xs[dc], 8), :]
         return part.reshape(RIM[k], 128).astype(BF16)
 
-    for k in range(8):
-        terms_s[k][...] = pack(cext, k, OUTER_Y, OUTER_X)
-    terms_x.start()
+    def send_terms(which):
+        for k in which:
+            terms_s[k][...] = pack(cext, k, OUTER_Y, OUTER_X)
+        terms_x.start(which)
+
+    def decode(p, carry):
+        zero = lax.shift_right_logical(p, 4)
+        for q in range(PC):
+            pos = PC * p + q
+            terms = jnp.dot(wt[pos], hid_out[pos], preferred_element_type=F32)
+            unpatch(cext, terms, p, zero + (8 + S * q))
+        return carry
+
+    lax.fori_loop(0, PR // 2, decode, 0)
+    send_terms([k for k in range(8) if DIRS[k][0] < 0])
+    lax.fori_loop(PR // 2, PR, decode, 0)
+    send_terms([k for k in range(8) if DIRS[k][0] >= 0])
 
     hidden_x.arrive()
 

time: 53.2 us -> 52.5 us (0.987)
  Pallas kernels: 52.7 us -> 51.8 us
    pallas_call x1, Pallas kernels: 49.1 us -> 48.3 us  [main_call(): pl.pallas_call(main_kernel, name='rica_main', out_shape=(pltpu.VMEM((n_po...]
where the time goes in v6:
time: 52.5 us; the launch traced here: 51.8 us
  Pallas kernels  51.8 us (99%)
    pallas_call x1, Pallas kernels, main_call(): pl.pallas_call(main_kernel, name='rica_main', out_shape=(pltpu.VMEM((n_po...  48.3 us
    pallas_call x1, Pallas kernels, grad_call(): pl.pallas_call(grad_kernel, name='rica_grad', out_shape=jax.ShapeDtypeStr...  3.51 us

profile of v6, /device:TPU:97, one launch (start us, length us, event | category | flops | bytes accessed | tf_op | source)
XLA Modules:
  0.0 51.8 jit_solution(13078711697113606604)
XLA Ops:
  0.0 48.3 %rica_main.1 = (bf16[12,1200,128]{2,1,0:T(8,128)(2,1)S(1)}, bf16[12,1200,128]{2,1,0:T(8,128)(2,1)S(1)}, bf16[12,128,128]{2,1,0:T(8,128)(2,1)S(1)}, bf16[12,128,128]{2,1,0:T(8,128)(2,1)S(1)}) custom-call(bf16[3,192,128]{2,1,0:T(8,128)(2,1)} %bitcast.10, bf16[12,1200,128]{2,1,0:T(8,128)(2,1)} %bitcast.9), custom_call_target="tpu_custom_call" | custom-call | tf_op jit(solution)/shard_map/rica_main/pallas_call | solution.py:591
  48.3 3.5 %rica_grad.1 = f32[12,1200,128]{2,1,0:T(8,128)} custom-call(bf16[12,1200,128]{2,1,0:T(8,128)(2,1)S(1)} %get-tuple-element.9.pat, bf16[12,1200,128]{2,1,0:T(8,128)(2,1)S(1)} %get-tuple-element.10.rpat, bf16[12,128,128]{2,1,0:T(8,128)(2,1)S(1)} %get-tuple-element.11.back, bf16[12,128,128]{2,1,0:T(8,128)(2,1)S(1)} %get-tuple-element.12.hid), custom_call_target="tpu_custom_call" | custom-call | tf_op jit(solution)/shard_map/rica_grad/pallas_call | solution.py:633

commit v7 on v6

--- a/solution.py
+++ b/solution.py
@@ -143,8 +143,7 @@
                 send_block(c, tr, (col + j) & (COLS - 1))
             return carry
 
-        lax.fori_loop(2, ROWS, send_row, 0)
-        send_row(1, 0)
+        lax.fori_loop(1, ROWS, send_row, 0)
         for j in range(1, COLS):
             send_block(c, row, (col + j) & (COLS - 1))
 

time: 52.5 us -> 52.1 us (level); the launches traced: 51.8 us -> 52 us
  no operation moved by 1% of the time
where the time goes in v7:
time: 52.1 us; the launch traced here: 52 us
  Pallas kernels  52 us (100%)
    pallas_call x1, Pallas kernels, main_call(): pl.pallas_call(main_kernel, name='rica_main', out_shape=(pltpu.VMEM((n_po...  48.5 us
    pallas_call x1, Pallas kernels, grad_call(): pl.pallas_call(grad_kernel, name='rica_grad', out_shape=jax.ShapeDtypeStr...  3.5 us

profile of v7, /device:TPU:97, one launch (start us, length us, event | category | flops | bytes accessed | tf_op | source)
XLA Modules:
  0.0 52.0 jit_solution(11651527644915069781)
XLA Ops:
  0.0 48.5 %rica_main.1 = (bf16[12,1200,128]{2,1,0:T(8,128)(2,1)S(1)}, bf16[12,1200,128]{2,1,0:T(8,128)(2,1)S(1)}, bf16[12,128,128]{2,1,0:T(8,128)(2,1)S(1)}, bf16[12,128,128]{2,1,0:T(8,128)(2,1)S(1)}) custom-call(bf16[3,192,128]{2,1,0:T(8,128)(2,1)} %bitcast.10, bf16[12,1200,128]{2,1,0:T(8,128)(2,1)} %bitcast.9), custom_call_target="tpu_custom_call" | custom-call | tf_op jit(solution)/shard_map/rica_main/pallas_call | solution.py:590
  48.5 3.5 %rica_grad.1 = f32[12,1200,128]{2,1,0:T(8,128)} custom-call(bf16[12,1200,128]{2,1,0:T(8,128)(2,1)S(1)} %get-tuple-element.9.pat, bf16[12,1200,128]{2,1,0:T(8,128)(2,1)S(1)} %get-tuple-element.10.rpat, bf16[12,128,128]{2,1,0:T(8,128)(2,1)S(1)} %get-tuple-element.11.back, bf16[12,128,128]{2,1,0:T(8,128)(2,1)S(1)} %get-tuple-element.12.hid), custom_call_target="tpu_custom_call" | custom-call | tf_op jit(solution)/shard_map/rica_grad/pallas_call | solution.py:632
